TPU v7x, 256 devices: a whole 4x4x8 slice. The times are simulated.
256 devices in a mesh: tile: 32 (over x_hi, z, core), wave: 8 (over x_lo, y).
Axes of the slice: x: 4 (x_hi: 2, x_lo: 2; x = x_hi * 2 + x_lo), y: 4, z: 8, core: 2. Of those that a mesh axis runs over, the one named last changes fastest.
Arguments:
- params: float32 [9, 512, 128], P(None, 'tile'), may hold values from -6 to 6
- dual_in: float32 [2, 9, 512, 128], P(None, None, 'tile'), may hold values from -4 to 4
- jacobian: bfloat16 [4, 9, 512, 128], P(None, None, 'tile'), may hold values from -3 to 3
- response: float32 [9, 256], P(None, 'wave'), may hold values from -5 to 5
- observed: bfloat16 [4, 256, 512, 128], P(None, 'wave', 'tile'), may hold values from -6 to 6
- psf: bfloat16 [17, 17], replicated, may hold values from -0.375 to 0.375
- step_size: float32 [], replicated, may hold values from 0.03 to 0.06
- dual_step: float32 [], replicated, may hold values from 0.5 to 1
- tv_bound: float32 [], replicated, may hold values from 1 to 2
- clip_bound: float32 [], replicated, may hold values from 0.5 to 1
Outputs:
- params_out: float32 [9, 512, 128], P(None, 'tile')
- dual_out: float32 [2, 9, 512, 128], P(None, None, 'tile')
- misfit: float32 [], replicated
All inputs are finite; a program needn't handle non-finite values.
Results may differ from a plain program's by a relative error of at most 0.0033.
Values may be sent and summed in bfloat16 or wider, within the bound.
No kernel may reach another device: no remote copies, remote signals or barrier semaphores. Data moves between devices by JAX's collectives and lax.ppermute only.
A program may use at most 128 MiB of HBM per device.

v0:
```python
import jax
import jax.numpy as jnp
from jax import lax
from jax.sharding import Mesh
from jax.sharding import PartitionSpec as P

TILE = ("tile_0", "tile_1", "tile_2")
WAVE = ("wave_0", "wave_1")
TILE_WAVE = ("tile_0", "tile_1", "tile_2", "wave_0", "wave_1")


def passed_along(x, axis, by):
    devices = lax.axis_size(axis)
    return lax.ppermute(x, axis, [(i, (i + by) % devices) for i in range(devices)])


def padded_2(block, sides, width):
    for axis, dim in sides:
        count = lax.axis_size(axis)
        forward = [(i, i + 1) for i in range(count - 1)]
        forward.append((count - 1, 0))
        backward = [(target, source) for source, target in forward]
        low = lax.ppermute(
            lax.slice_in_dim(block, block.shape[dim] - width, None, axis=dim), axis, forward
        )
        high = lax.ppermute(lax.slice_in_dim(block, 0, width, axis=dim), axis, backward)
        block = jnp.concatenate([low, block, high], axis=dim)
    return block


def by_axis(x, axes):
    for axis in axes:
        x = lax.psum(x, axis)
    return x


def sent_to_all(x, axis):
    devices = lax.axis_size(axis)
    return lax.all_to_all(jnp.broadcast_to(x[None], (devices, *x.shape)), axis, 0, 0, tiled=True)


def over_copies(x, axis):
    return sent_to_all(x, axis).sum(axis=0)


def toeplitz(psf, ncol):
    rows = jnp.arange(ncol, dtype=jnp.int32)[:, None]
    cols = jnp.arange(ncol, dtype=jnp.int32)[None, :]
    offset = (rows - cols + 8) % ncol
    onehot = (offset[None] == jnp.arange(17, dtype=jnp.int32)[:, None, None]).astype(jnp.float32)
    mats = jnp.einsum(
        "ab,bkj->akj", psf.astype(jnp.float32), onehot, precision=lax.Precision.HIGHEST
    )
    return mats.astype(jnp.bfloat16)


def blur_rows(padded, mats, adjoint):
    count = padded.shape[1] - 16
    total = jnp.zeros((padded.shape[0], count, padded.shape[2]), jnp.float32)
    for tap in range(17):
        window = padded[:, tap : tap + count]
        if adjoint:
            total = total + jnp.einsum(
                "nrk,jk->nrj", window, mats[16 - tap], preferred_element_type=jnp.float32
            )
        else:
            total = total + jnp.einsum(
                "nrk,kj->nrj", window, mats[tap], preferred_element_type=jnp.float32
            )
    return total


def synthesize(jac_band, state, response):
    terms = jac_band.astype(jnp.float32) * state[None]
    synthetic = jnp.einsum("pl,spij->slij", response, terms, precision=lax.Precision.HIGHEST)
    stokes, waves, rows, cols = synthetic.shape
    return synthetic.reshape(stokes * waves, rows, cols).astype(jnp.bfloat16)


def huber_total(resid, clip_bound):
    size = jnp.abs(resid)
    return jnp.sum(
        jnp.where(
            size <= clip_bound,
            0.5 * resid * resid,
            clip_bound * size - 0.5 * clip_bound * clip_bound,
        )
    )


def per_device(
    params, dual_in, jacobian, response, observed, psf, step_size, dual_step, tv_bound, clip_bound
):
    stokes, waves, rows, ncol = observed.shape
    images = stokes * waves
    mats = toeplitz(psf, ncol)
    flat_obs = observed.reshape(images, rows, ncol)
    following = passed_along(params[:, :1], TILE, -1)
    grad_r = jnp.concatenate([params[:, 1:], following], axis=1) - params
    grad_c = jnp.roll(params, -1, axis=2) - params
    dual_out = jnp.clip(dual_in + dual_step * jnp.stack([grad_r, grad_c]), -tv_bound, tv_bound)
    preceding = passed_along(dual_out[0][:, -1:], TILE, 1)
    divergence = dual_out[0] - jnp.concatenate([preceding, dual_out[0][:, :-1]], axis=1)
    divergence = divergence + (dual_out[1] - jnp.roll(dual_out[1], 1, axis=2))
    state = params
    misfit = jnp.float32(0.0)
    for step in range(2):
        synthetic = synthesize(jacobian, state, response)
        padded = padded_2(synthetic, ((TILE, 1),), 8)
        blurred = blur_rows(padded, mats, False)
        resid = blurred - flat_obs.astype(jnp.float32)
        huber = huber_total(resid, clip_bound)
        weighted = jnp.clip(resid, -clip_bound, clip_bound).astype(jnp.bfloat16)
        padded_back = padded_2(weighted, ((TILE, 1),), 8)
        back = blur_rows(padded_back, mats, True)
        along = jnp.einsum(
            "pl,slij->spij",
            response,
            back.reshape(stokes, waves, rows, ncol),
            precision=lax.Precision.HIGHEST,
        )
        partial_grad, huber = (jnp.sum(jacobian.astype(jnp.float32) * along, axis=0), huber)
        if step == 0:
            total_count = images * lax.axis_size(WAVE) * rows * lax.axis_size(TILE) * ncol
            misfit = by_axis(huber, TILE_WAVE) / total_count
        grad_now = over_copies(partial_grad, WAVE)
        state = state - step_size * (grad_now - divergence)
    return (state, dual_out, misfit)


def solution(mesh):
    split = Mesh(
        mesh.devices.reshape(2, 8, 2, 2, 4), ("tile_0", "tile_1", "tile_2", "wave_0", "wave_1")
    )
    placed = (
        P(None, TILE, None),
        P(None, None, TILE, None),
        P(None, None, TILE, None),
        P(None, WAVE),
        P(None, WAVE, TILE, None),
        P(),
        P(),
        P(),
        P(),
        P(),
    )
    return jax.shard_map(
        per_device,
        mesh=split,
        in_specs=placed,
        out_specs=(P(None, TILE, None), P(None, None, TILE, None), P()),
        check_vma=False,
    )
```

profile of v0, /device:TPU:2, one launch (start us, length us, event | category | flops | bytes accessed | tf_op | source)
XLA Modules:
  0.0 143.8 jit_solution(11062034957612363717)
XLA Ops:
  0.6 0.9 copy.58
  1.6 1.9 %fusion.64 = bf16[4,32,16,128]{3,1,2,0:T(8,128)(2,1)S(1)} fusion(bf16[4,9,16,128]{3,2,1,0:T(8,128)(2,1)} %param.12, f32[9,16,128]{2,0,1:T(8,128)S(1)} %copy.58, f32[9,32]{1,0:T(8,128)S(1)} %copy-done), kind=kOutput, calls=%fused_computation.76 | convolution fusion | flops 28721152 | bytes 746624 | tf_op jit(solution)/shard_map/pl,spij->slij/dot_general | solution.py:75
  3.8 0.7 copy.118
  4.5 0.7 copy.117
  5.3 6.9 %collective-permute-start.1 = (bf16[128,8,128]{2,0,1:T(8,128)(2,1)}, bf16[128,8,128]{2,0,1:T(8,128)(2,1)}, u32[]{:S(2)}, u32[]{:S(2)}) collective-permute-start(bf16[128,8,128]{2,0,1:T(8,128)(2,1)} %copy.117), channel_id=1, source_target_pairs={{8,0},{16,8},{24,16},{32,24},{40,32},{48,40},{56,48},{64,56},{72,6... | collective-permute-start | bytes 786440 | tf_op jit(solution)/shard_map/ppermute | solution.py:26
  12.1 0.6 slice.473
  12.7 0.7 collective-permute-start.4
  14.0 0.8 fusion.223
  17.7 1.0 constant_dynamic-update-slice_fusion.1
  20.9 1.0 constant_dynamic-update-slice_fusion.2
  23.9 0.6 fusion.61
  24.4 0.6 minimum_convert_fusion
  25.2 5.3 %collective-permute-start.3 = (bf16[128,8,128]{2,0,1:T(8,128)(2,1)S(1)}, bf16[128,8,128]{2,0,1:T(8,128)(2,1)S(1)}, u32[]{:S(2)}, u32[]{:S(2)}) collective-permute-start(bf16[128,8,128]{2,0,1:T(8,128)(2,1)S(1)} %get-tuple-element.29), channel_id=1, source_target_pairs={{8,0},{16,8},{24,16},{32,24},{40,32},{48,40},{56,48},{64,56},{72,6... | collective-permute-start | bytes 786440 | tf_op jit(solution)/shard_map/ppermute | solution.py:26
  30.9 3.7 %collective-permute-done.2 = bf16[128,8,128]{2,0,1:T(8,128)(2,1)S(1)} collective-permute-done((bf16[128,8,128]{2,0,1:T(8,128)(2,1)S(1)}, bf16[128,8,128]{2,0,1:T(8,128)(2,1)S(1)}, u32[]{:S(2)}, u32[]{:S(2)}) %collective-permute-start.2) | collective-permute-done | bytes 262176 | tf_op jit(solution)/shard_map/ppermute | solution.py:23
  38.8 0.6 fusion.46
  39.4 0.6 fusion.39
  40.3 0.7 fusion.68
  41.1 0.8 broadcast_in_dim.4
  41.9 5.8 %all-to-all-start = ((f32[8,9,16,128]{3,2,1,0:T(8,128)}), f32[8,9,16,128]{3,2,1,0:T(8,128)S(1)}, u32[]{:S(2)}, u32[]{:S(2)}) async-start(f32[8,9,16,128]{3,2,1,0:T(8,128)} %broadcast_in_dim.4), calls=%async_computation | async-start | bytes 1179648 | tf_op jit(solution)/shard_map/all_to_all | solution.py:39
  47.8 0.8 fusion.83
  48.5 0.9 fusion.82
  49.5 0.7 slice_bitcast_fusion.1
  50.2 1.4 slice.540
  52.2 1.6 %slice.543 = f32[9,16,1]{2,1,0:T(8,128)} slice(f32[9,16,128]{2,1,0:T(8,128)} %get-tuple-element.35), slice={[0:9], [0:16], [127:128]} | slice | bytes 1152 | tf_op jit(solution)/shard_map/jit(_roll_static)/slice | solution.py:104
  53.8 1.5 %all-to-all-done = f32[8,9,16,128]{3,2,1,0:T(8,128)S(1)} async-done(((f32[8,9,16,128]{3,2,1,0:T(8,128)}), f32[8,9,16,128]{3,2,1,0:T(8,128)S(1)}, u32[]{:S(2)}, u32[]{:S(2)}) %all-to-all-start) | async-done | bytes 589856 | tf_op jit(solution)/shard_map/all_to_all | solution.py:39
  55.3 0.7 reduce_sum.46
  56.0 2.5 %collective-permute-done.5 = f32[9,1,128]{2,1,0:T(1,128)} collective-permute-done((f32[9,1,128]{2,1,0:T(1,128)}, f32[9,1,128]{2,1,0:T(1,128)}, u32[]{:S(2)}, u32[]{:S(2)}) %collective-permute-start.5) | collective-permute-done | bytes 4640 | tf_op jit(solution)/shard_map/ppermute | solution.py:14
  58.5 1.1 multiply_subtract_fusion.1
  59.7 1.0 fusion.65
  61.2 5.4 %collective-permute-start.7 = (bf16[128,8,128]{2,0,1:T(8,128)(2,1)S(1)}, bf16[128,8,128]{2,0,1:T(8,128)(2,1)S(1)}, u32[]{:S(2)}, u32[]{:S(2)}) collective-permute-start(bf16[128,8,128]{2,0,1:T(8,128)(2,1)S(1)} %copy.119), channel_id=1, source_target_pairs={{8,0},{16,8},{24,16},{32,24},{40,32},{48,40},{56,48},{64,56},{72,6... | collective-permute-start | bytes 786440 | tf_op jit(solution)/shard_map/ppermute | solution.py:26
  66.9 3.6 %collective-permute-done.6 = bf16[128,8,128]{2,0,1:T(8,128)(2,1)S(1)} collective-permute-done((bf16[128,8,128]{2,0,1:T(8,128)(2,1)S(1)}, bf16[128,8,128]{2,0,1:T(8,128)(2,1)S(1)}, u32[]{:S(2)}, u32[]{:S(2)}) %collective-permute-start.6) | collective-permute-done | bytes 262176 | tf_op jit(solution)/shard_map/ppermute | solution.py:23
  74.2 0.5 copy-done.5
  75.3 0.5 fusion.32
  75.8 0.6 fusion.62
  76.8 5.3 %collective-permute-start.9 = (bf16[128,8,128]{2,0,1:T(8,128)(2,1)S(1)}, bf16[128,8,128]{2,0,1:T(8,128)(2,1)S(1)}, u32[]{:S(2)}, u32[]{:S(2)}) collective-permute-start(bf16[128,8,128]{2,0,1:T(8,128)(2,1)S(1)} %get-tuple-element.23), channel_id=1, source_target_pairs={{8,0},{16,8},{24,16},{32,24},{40,32},{48,40},{56,48},{64,56},{72,6... | collective-permute-start | bytes 786440 | tf_op jit(solution)/shard_map/ppermute | solution.py:26
  82.4 3.8 %collective-permute-done.8 = bf16[128,8,128]{2,0,1:T(8,128)(2,1)S(1)} collective-permute-done((bf16[128,8,128]{2,0,1:T(8,128)(2,1)S(1)}, bf16[128,8,128]{2,0,1:T(8,128)(2,1)S(1)}, u32[]{:S(2)}, u32[]{:S(2)}) %collective-permute-start.8) | collective-permute-done | bytes 262176 | tf_op jit(solution)/shard_map/ppermute | solution.py:23
  90.4 0.6 fusion.15
  91.0 0.6 fusion.8
  91.5 0.7 fusion.69
  92.3 0.8 broadcast_in_dim.5
  93.1 5.7 %all-to-all-start.1 = ((f32[8,9,16,128]{3,2,1,0:T(8,128)}), f32[8,9,16,128]{3,2,1,0:T(8,128)S(1)}, u32[]{:S(2)}, u32[]{:S(2)}) async-start(f32[8,9,16,128]{3,2,1,0:T(8,128)} %broadcast_in_dim.5), calls=%async_computation.1 | async-start | bytes 1179648 | tf_op jit(solution)/shard_map/all_to_all | solution.py:39
  98.9 0.9 fusion.71
  99.9 7.1 %psum.35 = f32[]{:T(128)} all-reduce(f32[]{:T(128)} %fusion.71), channel_id=1, replica_groups=mesh['tile_0'=2,'tile_1'=8,'tile_2'=2,'wave_0'=2,'wave_1'=4] {'tile_0'}, use_global_device_ids=true, to_apply=%region_5.6 | all-reduce | flops 1 | bytes 8 | tf_op jit(solution)/shard_map/psum | solution.py:33
  106.9 14.8 %psum.36 = f32[]{:T(128)} all-reduce(f32[]{:T(128)} %psum.35), channel_id=1, replica_groups=mesh['tile_0'=2,'tile_1'=8,'tile_2'=2,'wave_0'=2,'wave_1'=4] {'tile_1'}, use_global_device_ids=true, to_apply=%region_6.7 | all-reduce | flops 1 | bytes 8 | tf_op jit(solution)/shard_map/psum | solution.py:33
  121.7 3.1 %psum.37 = f32[]{:T(128)} all-reduce(f32[]{:T(128)} %psum.36), channel_id=1, replica_groups=mesh['tile_0'=2,'tile_1'=8,'tile_2'=2,'wave_0'=2,'wave_1'=4] {'tile_2'}, use_global_device_ids=true, to_apply=%region_7.8 | all-reduce | flops 1 | bytes 8 | tf_op jit(solution)/shard_map/psum | solution.py:33
  124.8 5.6 %psum.38 = f32[]{:T(128)} all-reduce(f32[]{:T(128)} %psum.37), channel_id=1, replica_groups=mesh['tile_0'=2,'tile_1'=8,'tile_2'=2,'wave_0'=2,'wave_1'=4] {'wave_0'}, use_global_device_ids=true, to_apply=%region_8.9 | all-reduce | flops 1 | bytes 8 | tf_op jit(solution)/shard_map/psum | solution.py:33
  130.3 11.0 %psum.39 = f32[]{:T(128)} all-reduce(f32[]{:T(128)} %psum.38), channel_id=1, replica_groups=mesh['tile_0'=2,'tile_1'=8,'tile_2'=2,'wave_0'=2,'wave_1'=4] {'wave_1'}, use_global_device_ids=true, to_apply=%region_9.10 | all-reduce | flops 1 | bytes 8 | tf_op jit(solution)/shard_map/psum | solution.py:33
  142.0 0.7 multiply_subtract_fusion
  (130 shorter events, 20.7 us)
Async XLA Ops:
  0.6 0.9 copy-start
  3.7 8.4 %copy-start.2 = (f32[9,16,128]{2,1,0:T(8,128)S(1)}, f32[9,16,128]{2,1,0:T(8,128)}, u32[]{:S(2)}) copy-start(f32[9,16,128]{2,1,0:T(8,128)} %param.10) | copy-start | bytes 221188
  3.7 9.8 %copy-start.9 = (bf16[17,17]{1,0:T(8,128)(2,1)S(1)}, bf16[17,17]{1,0:T(8,128)(2,1)}, u32[]{:S(2)}) copy-start(bf16[17,17]{1,0:T(8,128)(2,1)} %param.15) | copy-start | bytes 1738
  4.5 13.1 %collective-permute-start = (bf16[128,8,128]{2,0,1:T(8,128)(2,1)}, bf16[128,8,128]{2,0,1:T(8,128)(2,1)}, u32[]{:S(2)}, u32[]{:S(2)}) collective-permute-start(bf16[128,8,128]{2,0,1:T(8,128)(2,1)} %copy.118), channel_id=1, source_target_pairs={{0,8},{8,16},{16,24},{24,32},{32,40},{40,48},{48,56},{56,64},{64,7... | collective-permute-start | bytes 786440 | tf_op jit(solution)/shard_map/ppermute | solution.py:23
  5.3 15.6 %collective-permute-start.1 = (bf16[128,8,128]{2,0,1:T(8,128)(2,1)}, bf16[128,8,128]{2,0,1:T(8,128)(2,1)}, u32[]{:S(2)}, u32[]{:S(2)}) collective-permute-start(bf16[128,8,128]{2,0,1:T(8,128)(2,1)} %copy.117), channel_id=1, source_target_pairs={{8,0},{16,8},{24,16},{32,24},{40,32},{48,40},{56,48},{64,56},{72,6... | collective-permute-start | bytes 786440 | tf_op jit(solution)/shard_map/ppermute | solution.py:26
  12.7 35.0 %collective-permute-start.4 = (f32[9,1,128]{2,1,0:T(1,128)}, f32[9,1,128]{2,1,0:T(1,128)}, u32[]{:S(2)}, u32[]{:S(2)}) collective-permute-start(f32[9,1,128]{2,1,0:T(1,128)} %slice.473), channel_id=1, source_target_pairs={{0,248},{8,0},{16,8},{24,16},{32,24},{40,32},{48,40},{56,48},{64,5... | collective-permute-start | bytes 13832 | tf_op jit(solution)/shard_map/ppermute | solution.py:14
  14.9 1.1 copy-start.8
  15.0 15.6 %copy-start.6 = (bf16[1,128,128]{2,1,0:T(8,128)(2,1)}, bf16[1,128,128]{2,1,0:T(8,128)(2,1)S(1)}, u32[]{:S(2)}) copy-start(bf16[1,128,128]{2,1,0:T(8,128)(2,1)S(1)} %copy.86) | copy-start | bytes 98308
  15.1 19.5 %copy-start.4 = (bf16[1,128,128]{2,1,0:T(8,128)(2,1)}, bf16[1,128,128]{2,1,0:T(8,128)(2,1)S(1)}, u32[]{:S(2)}) copy-start(bf16[1,128,128]{2,1,0:T(8,128)(2,1)S(1)} %copy.93) | copy-start | bytes 98308
  25.1 9.5 %collective-permute-start.2 = (bf16[128,8,128]{2,0,1:T(8,128)(2,1)S(1)}, bf16[128,8,128]{2,0,1:T(8,128)(2,1)S(1)}, u32[]{:S(2)}, u32[]{:S(2)}) collective-permute-start(bf16[128,8,128]{2,0,1:T(8,128)(2,1)S(1)} %get-tuple-element.28), channel_id=1, source_target_pairs={{0,8},{8,16},{16,24},{24,32},{32,40},{40,48},{48,56},{56,64},{64,7... | collective-permute-start | bytes 786440 | tf_op jit(solution)/shard_map/ppermute | solution.py:23
  25.2 11.5 %collective-permute-start.3 = (bf16[128,8,128]{2,0,1:T(8,128)(2,1)S(1)}, bf16[128,8,128]{2,0,1:T(8,128)(2,1)S(1)}, u32[]{:S(2)}, u32[]{:S(2)}) collective-permute-start(bf16[128,8,128]{2,0,1:T(8,128)(2,1)S(1)} %get-tuple-element.29), channel_id=1, source_target_pairs={{8,0},{16,8},{24,16},{32,24},{40,32},{48,40},{56,48},{64,56},{72,6... | collective-permute-start | bytes 786440 | tf_op jit(solution)/shard_map/ppermute | solution.py:26
  39.4 0.9 copy-start.1
  41.9 13.4 %all-to-all-start = ((f32[8,9,16,128]{3,2,1,0:T(8,128)}), f32[8,9,16,128]{3,2,1,0:T(8,128)S(1)}, u32[]{:S(2)}, u32[]{:S(2)}) async-start(f32[8,9,16,128]{3,2,1,0:T(8,128)} %broadcast_in_dim.4), calls=%async_computation | async-start | bytes 1179648 | tf_op jit(solution)/shard_map/all_to_all | solution.py:39
  49.5 11.2 %copy-start.3 = (f32[2,9,16,128]{3,2,1,0:T(8,128)}, f32[2,9,16,128]{3,2,1,0:T(8,128)S(1)}, u32[]{:S(2)}) copy-start(f32[2,9,16,128]{3,2,1,0:T(8,128)S(1)} %fusion.82) | copy-start | bytes 442372
  51.6 7.0 %collective-permute-start.5 = (f32[9,1,128]{2,1,0:T(1,128)}, f32[9,1,128]{2,1,0:T(1,128)}, u32[]{:S(2)}, u32[]{:S(2)}) collective-permute-start(f32[9,1,128]{2,1,0:T(1,128)} %slice.540), channel_id=1, source_target_pairs={{0,8},{8,16},{16,24},{24,32},{32,40},{40,48},{48,56},{56,64},{64,7... | collective-permute-start | bytes 13832 | tf_op jit(solution)/shard_map/ppermute | solution.py:14
  60.9 5.7 %copy-start.7 = (bf16[1,128,128]{2,1,0:T(8,128)(2,1)S(1)}, bf16[1,128,128]{2,1,0:T(8,128)(2,1)}, u32[]{:S(2)}) copy-start(bf16[1,128,128]{2,1,0:T(8,128)(2,1)} %copy-done.6) | copy-start | bytes 98308
  61.0 9.5 %collective-permute-start.6 = (bf16[128,8,128]{2,0,1:T(8,128)(2,1)S(1)}, bf16[128,8,128]{2,0,1:T(8,128)(2,1)S(1)}, u32[]{:S(2)}, u32[]{:S(2)}) collective-permute-start(bf16[128,8,128]{2,0,1:T(8,128)(2,1)S(1)} %copy.120), channel_id=1, source_target_pairs={{0,8},{8,16},{16,24},{24,32},{32,40},{40,48},{48,56},{56,64},{64,7... | collective-permute-start | bytes 786440 | tf_op jit(solution)/shard_map/ppermute | solution.py:23
  61.2 11.6 %collective-permute-start.7 = (bf16[128,8,128]{2,0,1:T(8,128)(2,1)S(1)}, bf16[128,8,128]{2,0,1:T(8,128)(2,1)S(1)}, u32[]{:S(2)}, u32[]{:S(2)}) collective-permute-start(bf16[128,8,128]{2,0,1:T(8,128)(2,1)S(1)} %copy.119), channel_id=1, source_target_pairs={{8,0},{16,8},{24,16},{32,24},{40,32},{48,40},{56,48},{64,56},{72,6... | collective-permute-start | bytes 786440 | tf_op jit(solution)/shard_map/ppermute | solution.py:26
  74.0 0.8 copy-start.5
  76.5 9.7 %collective-permute-start.8 = (bf16[128,8,128]{2,0,1:T(8,128)(2,1)S(1)}, bf16[128,8,128]{2,0,1:T(8,128)(2,1)S(1)}, u32[]{:S(2)}, u32[]{:S(2)}) collective-permute-start(bf16[128,8,128]{2,0,1:T(8,128)(2,1)S(1)} %get-tuple-element.22), channel_id=1, source_target_pairs={{0,8},{8,16},{16,24},{24,32},{32,40},{40,48},{48,56},{56,64},{64,7... | collective-permute-start | bytes 786440 | tf_op jit(solution)/shard_map/ppermute | solution.py:23
  76.8 11.5 %collective-permute-start.9 = (bf16[128,8,128]{2,0,1:T(8,128)(2,1)S(1)}, bf16[128,8,128]{2,0,1:T(8,128)(2,1)S(1)}, u32[]{:S(2)}, u32[]{:S(2)}) collective-permute-start(bf16[128,8,128]{2,0,1:T(8,128)(2,1)S(1)} %get-tuple-element.23), channel_id=1, source_target_pairs={{8,0},{16,8},{24,16},{32,24},{40,32},{48,40},{56,48},{64,56},{72,6... | collective-permute-start | bytes 786440 | tf_op jit(solution)/shard_map/ppermute | solution.py:26
  93.1 48.9 %all-to-all-start.1 = ((f32[8,9,16,128]{3,2,1,0:T(8,128)}), f32[8,9,16,128]{3,2,1,0:T(8,128)S(1)}, u32[]{:S(2)}, u32[]{:S(2)}) async-start(f32[8,9,16,128]{3,2,1,0:T(8,128)} %broadcast_in_dim.5), calls=%async_computation.1 | async-start | bytes 1179648 | tf_op jit(solution)/shard_map/all_to_all | solution.py:39
where the time goes:
time: 145 us; the launch traced here: 144 us
  blocking collectives  41.5 us (29%)
  starting transfers between devices  35.6 us (25%)
  matrix products  26.8 us (18%)
  waiting for transfers between devices  15.2 us (10%)
  local copies, waits for them, and re-layouts  13.7 us (9%)
  between operations  5.74 us (4%)
  other arithmetic  5.3 us (4%)
    psum x5, blocking collectives, by_axis(): x = lax.psum(x, axis)  41.5 us
    ppermute x4, starting transfers between devices, padded_2(): lax.ppermute(lax.slice_in_dim(block, 0, width, axis=dim), axis, backward)  23 us
    all_to_all x2, starting transfers between devices, sent_to_all(): lax.all_to_all(jnp.broadcast_to(x[None], (devices, *x.shape)), axis, 0, 0...  11.5 us
    dot_general x34, matrix products, blur_rows(): jnp.einsum('nrk,jk->nrj', window, mats[16 - tap], preferred_element_type=...  11.2 us
    ppermute x4, waiting for transfers between devices, padded_2(): lax.ppermute(lax.slice_in_dim(block, block.shape[dim] - width, None, axis...  11.2 us
    dot_general x34, matrix products, blur_rows(): jnp.einsum('nrk,kj->nrj', window, mats[tap], preferred_element_type=jnp.f...  10.8 us
    unnamed x44, local copies, waits for them, and re-layouts  4.53 us
    dot_general x2, matrix products, synthesize(): jnp.einsum('pl,spij->slij', response, terms, precision=lax.Precision.HIGH...  2.96 us
  transfers between devices with their start and end apart: 12, of which 5 were waited for; matrix products, arithmetic and copies ran while one was open for 21% of the time, Pallas kernels for 0%

commit v1 on v0

v1 whole, which is shorter than its diff:
```python
import functools

import jax
import jax.numpy as jnp
from jax import lax
from jax.experimental import pallas as pl
from jax.experimental.pallas import tpu as pltpu
from jax.sharding import Mesh
from jax.sharding import PartitionSpec as P

TILE = ("tile_0", "tile_1", "tile_2")
WAVE = ("wave_0", "wave_1")
ALL = TILE + WAVE
F32 = jnp.float32
BF16 = jnp.bfloat16

SP = 36
SPP = 40
HL = 2 * SPP
TAPS = 17
PAIRS = 9


def passed_along(x, axis, by):
    devices = lax.axis_size(axis)
    return lax.ppermute(x, axis, [(i, (i + by) % devices) for i in range(devices)])


def split_rows(value):
    high = value.astype(BF16).astype(F32)
    return jnp.concatenate([high, value - high], axis=0).astype(BF16)


def weights_kernel(psf_ref, forward_ref, adjoint_ref):
    n = 128
    row = lax.broadcasted_iota(jnp.int32, (n, n), 0)
    col = lax.broadcasted_iota(jnp.int32, (n, n), 1)
    offset = lax.rem(row - col + (n + 8), n)
    zero = jnp.zeros((n, n), BF16)
    for ref in (forward_ref, adjoint_ref):
        ref[0:n, n : 2 * n] = zero
        ref[TAPS * n : (TAPS + 1) * n, 0:n] = zero
    for tap in range(TAPS):
        for ref, flip in ((forward_ref, False), (adjoint_ref, True)):
            mat = jnp.zeros((n, n), F32)
            for b in range(TAPS):
                scalar = psf_ref[16 - tap, 16 - b] if flip else psf_ref[tap, b]
                mat = jnp.where(offset == b, scalar, mat)
            mat = mat.astype(BF16)
            ref[tap * n : (tap + 1) * n, 0:n] = mat
            ref[(tap + 1) * n : (tap + 2) * n, n : 2 * n] = mat


def step_kernel(
    clip_ref,
    x_lo, x_own, x_hi,
    j_lo, j_own, j_hi,
    o_lo, o_own, o_hi,
    resp_ref, resp_t_ref,
    forward_ref, adjoint_ref,
    out_ref,
    terms, stacked, obs, contracted, along,
):
    n = 128
    clip = clip_ref[0]
    terms[SP * 48 : SPP * 48, :] = jnp.zeros(((SPP - SP) * 48, n), F32)
    for part, (x_ref, j_ref) in enumerate(((x_lo, j_lo), (x_own, j_own), (x_hi, j_hi))):
        for image in range(SP):
            terms[image * 48 + part * 16 : image * 48 + part * 16 + 16, :] = (
                j_ref[image].astype(F32) * x_ref[image % 9]
            )
    obs[:, 0:8, :] = o_lo[...].astype(F32)
    obs[:, 8:24, :] = o_own[...].astype(F32)
    obs[:, 24:32, :] = o_hi[...].astype(F32)
    obs_flat = obs.reshape(128 * 32, n)
    for row in range(48):
        pair, half = row // 2, row % 2
        stacked[pair * HL : (pair + 1) * HL, half * n : (half + 1) * n] = split_rows(
            terms[pl.ds(row, SPP, stride=48), :]
        )
    huber = jnp.zeros((8, 2 * n), F32)
    for block in range(4):
        windows = [
            stacked[(4 * block + k) * HL : (4 * block + k + 4) * HL, :] for k in range(PAIRS)
        ]
        blurred = jnp.dot(
            jnp.concatenate(windows, axis=1), forward_ref[...], preferred_element_type=F32
        )
        for i in range(4):
            pair = 4 * block + i
            model = blurred[i * HL : i * HL + SPP] + blurred[i * HL + SPP : (i + 1) * HL]
            high = model.astype(BF16).astype(F32)
            model = jnp.concatenate(
                [high, model - high, high, jnp.zeros((8, 2 * n), F32)], axis=0
            ).astype(BF16)
            seen = jnp.concatenate(
                [
                    obs_flat[pl.ds(2 * pair, 128, stride=32), :],
                    obs_flat[pl.ds(2 * pair + 1, 128, stride=32), :],
                ],
                axis=1,
            )
            resid = jnp.dot(resp_ref[...], model, preferred_element_type=F32) - seen
            weighted = jnp.clip(resid, -clip, clip)
            if 4 <= pair < 12:
                loss = weighted * (resid - 0.5 * weighted)
                huber = huber + jnp.sum(loss.reshape(16, 8, 2 * n), axis=0)
            summed = jnp.dot(
                resp_t_ref[...], weighted.astype(BF16), preferred_element_type=F32
            )
            contracted[pair * HL : (pair + 1) * HL, :] = split_rows(
                summed[:SPP] + summed[SPP:]
            )
    for block in range(2):
        windows = [
            contracted[(4 * block + k) * HL : (4 * block + k + 4) * HL, :] for k in range(PAIRS)
        ]
        back = jnp.dot(
            jnp.concatenate(windows, axis=1), adjoint_ref[...], preferred_element_type=F32
        )
        for i in range(4):
            pair = 4 * block + i
            both = back[i * HL : i * HL + SPP] + back[i * HL + SPP : (i + 1) * HL]
            along[pl.ds(2 * pair, SPP, stride=16), :] = both[:, :n]
            along[pl.ds(2 * pair + 1, SPP, stride=16), :] = both[:, n:]
    for p in range(9):
        total = jnp.zeros((16, n), F32)
        for s in range(4):
            image = s * 9 + p
            total = total + j_own[image].astype(F32) * along[image * 16 : image * 16 + 16, :]
        for copy in range(8):
            out_ref[copy, p * 16 : p * 16 + 16, :] = total
    for copy in range(8):
        out_ref[copy, 144:152, :] = huber[:, :n] + huber[:, n:]


def vmem_specs(count):
    return [pl.BlockSpec(memory_space=pltpu.VMEM) for _ in range(count)]


def blur_weights(psf):
    shape = jax.ShapeDtypeStruct((18 * 128, 256), BF16)
    return pl.pallas_call(
        weights_kernel,
        out_shape=(shape, shape),
        in_specs=[pl.BlockSpec(memory_space=pltpu.SMEM)],
        out_specs=tuple(vmem_specs(2)),
        name="blur_weights",
    )(psf.astype(F32))


def partial_gradient(clip_bound, x, jac, obs, resp, resp_t, forward, adjoint):
    return pl.pallas_call(
        step_kernel,
        out_shape=jax.ShapeDtypeStruct((8, 152, 128), F32),
        in_specs=[pl.BlockSpec(memory_space=pltpu.SMEM)] + vmem_specs(13),
        out_specs=pl.BlockSpec(memory_space=pltpu.VMEM),
        scratch_shapes=[
            pltpu.VMEM((SPP * 48, 128), F32),
            pltpu.VMEM((24 * HL, 256), BF16),
            pltpu.VMEM((128, 32, 128), F32),
            pltpu.VMEM((16 * HL, 256), BF16),
            pltpu.VMEM((SPP * 16, 128), F32),
        ],
        compiler_params=pltpu.CompilerParams(vmem_limit_bytes=40 * 1024 * 1024),
        cost_estimate=pl.CostEstimate(
            flops=3_000_000_000, bytes_accessed=6_000_000, transcendentals=0
        ),
        name="partial_gradient",
    )(clip_bound.reshape(1), *x, *jac, *obs, resp, resp_t, forward, adjoint)


def response_matrices(response):
    block = jnp.einsum("st,pl->sltp", jnp.eye(4, dtype=F32), response).reshape(128, SP)
    block = jnp.pad(block, ((0, 0), (0, SPP - SP)))
    high = block.astype(BF16).astype(F32)
    low = block - high
    forward = jnp.concatenate([high, high, low, jnp.zeros((128, 8), F32)], axis=1)
    backward = jnp.concatenate([high.T, low.T], axis=0)
    return forward.astype(BF16), backward.astype(BF16)


def per_device(
    params, dual_in, jacobian, response, observed, psf, step_size, dual_step, tv_bound, clip_bound
):
    stokes, waves, rows, ncol = observed.shape
    jac = jacobian.reshape(SP, rows, ncol)
    obs = observed.reshape(stokes * waves, rows, ncol)
    x_lo, x_hi = passed_along(params, TILE, 1), passed_along(params, TILE, -1)
    j_lo, j_hi = passed_along(jac, TILE, 1), passed_along(jac, TILE, -1)
    o_lo = passed_along(obs[:, rows - 8 :], TILE, 1)
    o_hi = passed_along(obs[:, :8], TILE, -1)
    jac = (j_lo, jac, j_hi)
    obs = (o_lo, obs, o_hi)
    forward, adjoint = blur_weights(psf)
    resp, resp_t = response_matrices(response)

    grad_r = jnp.concatenate([params[:, 1:], x_hi[:, :1]], axis=1) - params
    grad_c = jnp.roll(params, -1, axis=2) - params
    dual_out = jnp.clip(dual_in + dual_step * jnp.stack([grad_r, grad_c]), -tv_bound, tv_bound)
    preceding = passed_along(dual_out[0][:, -1:], TILE, 1)
    divergence = dual_out[0] - jnp.concatenate([preceding, dual_out[0][:, :-1]], axis=1)
    divergence = divergence + (dual_out[1] - jnp.roll(dual_out[1], 1, axis=2))

    part = partial_gradient(clip_bound, (x_lo, params, x_hi), jac, obs, resp, resp_t, forward, adjoint)
    whole = lax.all_to_all(part, WAVE, 0, 0, tiled=True).sum(axis=0)
    state = params - step_size * (whole[:144].reshape(9, rows, ncol) - divergence)
    loss = whole[144:]

    x_lo, x_hi = passed_along(state, TILE, 1), passed_along(state, TILE, -1)
    tiles, wavs = lax.axis_size(TILE), lax.axis_size(WAVE)
    each = tiles // wavs
    losses = [
        lax.ppermute(
            loss,
            ALL,
            [
                (((t + each * w + k) % tiles) * wavs + w, t * wavs + w)
                for t in range(tiles)
                for w in range(wavs)
            ],
        )
        for k in range(each)
    ]
    loss = sum(losses[1:], losses[0])
    part = partial_gradient(clip_bound, (x_lo, state, x_hi), jac, obs, resp, resp_t, forward, adjoint)
    part = part.at[:, 144:].set(jnp.broadcast_to(loss, (8, 8, ncol)))
    whole = lax.all_to_all(part, WAVE, 0, 0, tiled=True).sum(axis=0)
    state = state - step_size * (whole[:144].reshape(9, rows, ncol) - divergence)
    total = stokes * waves * wavs * rows * tiles * ncol
    misfit = jnp.sum(whole[144:]) / total
    return (state, dual_out, misfit)


def solution(mesh):
    split = Mesh(
        mesh.devices.reshape(2, 8, 2, 2, 4), ("tile_0", "tile_1", "tile_2", "wave_0", "wave_1")
    )
    placed = (
        P(None, TILE, None),
        P(None, None, TILE, None),
        P(None, None, TILE, None),
        P(None, WAVE),
        P(None, WAVE, TILE, None),
        P(),
        P(),
        P(),
        P(),
        P(),
    )
    return jax.shard_map(
        per_device,
        mesh=split,
        in_specs=placed,
        out_specs=(P(None, TILE, None), P(None, None, TILE, None), P()),
        check_vma=False,
    )
```

time: 145 us -> 104 us (0.72)
  the two profiles are of different devices: /device:TPU:2 before, /device:TPU:65 now
where the time goes in v1:
time: 104 us; the launch traced here: 103 us
  starting transfers between devices  29.4 us (28%)
  blocking collectives  24.2 us (23%)
  Pallas kernels  19.2 us (18%)
  local copies, waits for them, and re-layouts  10.6 us (10%)
  other arithmetic  7.46 us (7%)
  waiting for transfers between devices  7.2 us (7%)
  between operations  5.32 us (5%)
    all_to_all x1, blocking collectives, per_device(): whole = lax.all_to_all(part, WAVE, 0, 0, tiled=True).sum(axis=0)  24.2 us
    ppermute x4, starting transfers between devices, per_device(): lax.ppermute(loss, ALL, [((t + each * w + k) % tiles * wavs + w, t * wavs...  14.7 us
    pallas_call x2, Pallas kernels, partial_gradient(): pl.pallas_call(step_kernel, out_shape=jax.ShapeDtypeStruct((8, 152, 128),...  14.4 us
    ppermute x9, starting transfers between devices, passed_along(): lax.ppermute(x, axis, [(i, (i + by) % devices) for i in range(devices)])  9.6 us
    unnamed x36, local copies, waits for them, and re-layouts  6.77 us
    ppermute x9, waiting for transfers between devices, passed_along(): lax.ppermute(x, axis, [(i, (i + by) % devices) for i in range(devices)])  5.15 us
    all_to_all x1, starting transfers between devices, per_device(): whole = lax.all_to_all(part, WAVE, 0, 0, tiled=True).sum(axis=0)  5.13 us
    pallas_call x1, Pallas kernels, blur_weights(): pl.pallas_call(weights_kernel, out_shape=(shape, shape), in_specs=[pl.Blo...  4.78 us
  transfers between devices with their start and end apart: 14, of which 4 were waited for; matrix products, arithmetic and copies ran while one was open for 10% of the time, Pallas kernels for 5%

profile of v1, /device:TPU:65, one launch (start us, length us, event | category | flops | bytes accessed | tf_op | source)
XLA Modules:
  0.0 103.3 jit_solution(16228966053970978163)
XLA Ops:
  0.7 0.0 copy-start
  0.7 2.3 %collective-permute-start.2 = (bf16[36,16,128]{2,1,0:T(8,128)(2,1)}, bf16[36,16,128]{2,1,0:T(8,128)(2,1)S(1)}, u32[]{:S(2)}, u32[]{:S(2)}) collective-permute-start(bf16[36,16,128]{2,1,0:T(8,128)(2,1)} %bitcast.36), channel_id=1, source_target_pairs={{0,8},{8,16},{16,24},{24,32},{32,40},{40,48},{48,56},{56,64},{64,7... | collective-permute-start | bytes 442376 | tf_op jit(solution)/shard_map/ppermute | solution.py:26
  3.0 1.1 %fusion.9 = (bf16[128,8,128]{2,1,0:T(8,128)(2,1)S(1)}, bf16[128,8,128]{2,1,0:T(8,128)(2,1)S(1)}) fusion(bf16[128,16,128]{2,1,0:T(8,128)(2,1)} %bitcast.33), kind=kLoop, calls=%fused_computation.26 | loop fusion | bytes 1048576 | tf_op jit(solution)/shard_map/slice | solution.py:192
  4.0 1.8 %collective-permute-start.4 = (bf16[128,8,128]{2,1,0:T(8,128)(2,1)S(1)}, bf16[128,8,128]{2,1,0:T(8,128)(2,1)S(1)}, u32[]{:S(2)}, u32[]{:S(2)}) collective-permute-start(bf16[128,8,128]{2,1,0:T(8,128)(2,1)S(1)} %get-tuple-element.22), channel_id=1, source_target_pairs={{0,8},{8,16},{16,24},{24,32},{32,40},{40,48},{48,56},{56,64},{64,7... | collective-permute-start | bytes 786440 | tf_op jit(solution)/shard_map/ppermute | solution.py:26
  5.8 0.0 collective-permute-start.5
  5.8 0.2 collective-permute-start.1
  6.1 0.8 multiply_bitcast_fusion
  6.8 0.1 reshape.57
  7.0 0.1 pad.22.clone
  7.1 0.1 maximum_maximum_fusion
  7.2 0.1 slice.82
  7.3 0.1 copy.13.resp_ref
  7.4 0.6 convert_element_type.16.psf_ref
  8.0 4.8 %blur_weights.1 = (bf16[2304,256]{1,0:T(8,128)(2,1)}, bf16[2304,256]{1,0:T(8,128)(2,1)}) custom-call(f32[17,17]{1,0:T(8,128)} %convert_element_type.16.psf_ref), custom_call_target="tpu_custom_call" | custom-call | tf_op jit(solution)/shard_map/blur_weights/pallas_call | solution.py:143
  14.8 1.8 %collective-permute-start = (f32[9,16,128]{2,1,0:T(8,128)S(1)}, f32[9,16,128]{2,1,0:T(8,128)S(1)}, u32[]{:S(2)}, u32[]{:S(2)}) collective-permute-start(f32[9,16,128]{2,1,0:T(8,128)S(1)} %copy-done), channel_id=1, source_target_pairs={{0,8},{8,16},{16,24},{24,32},{32,40},{40,48},{48,56},{56,64},{64,7... | collective-permute-start | bytes 221192 | tf_op jit(solution)/shard_map/ppermute | solution.py:26
  16.6 1.4 %collective-permute-done.x_lo = f32[9,16,128]{2,1,0:T(8,128)S(1)} collective-permute-done((f32[9,16,128]{2,1,0:T(8,128)S(1)}, f32[9,16,128]{2,1,0:T(8,128)S(1)}, u32[]{:S(2)}, u32[]{:S(2)}) %collective-permute-start) | collective-permute-done | bytes 73760 | tf_op jit(solution)/shard_map/ppermute | solution.py:26
  18.1 1.4 %copy-done.2 = bf16[2304,256]{1,0:T(8,128)(2,1)S(1)} copy-done((bf16[2304,256]{1,0:T(8,128)(2,1)S(1)}, bf16[2304,256]{1,0:T(8,128)(2,1)}, u32[]{:S(2)}) %copy-start.2) | copy-done | bytes 1179672
  19.5 1.3 %copy-done.4 = bf16[2304,256]{1,0:T(8,128)(2,1)S(1)} copy-done((bf16[2304,256]{1,0:T(8,128)(2,1)S(1)}, bf16[2304,256]{1,0:T(8,128)(2,1)}, u32[]{:S(2)}) %copy-start.4) | copy-done | bytes 1179672
  20.7 7.6 %partial_gradient.2 = f32[8,152,128]{2,1,0:T(8,128)} custom-call(f32[1]{0:T(128)} %bitcast.30.clip_ref, f32[9,16,128]{2,1,0:T(8,128)S(1)} %collective-permute-done.x_lo, f32[9,16,128]{2,1,0:T(8,128)S(1)} %copy-done, f32[9,16,128]{2,1,0:T(8,128)S(1)} %collective-permute-done.1.x_hi, bf16[36,16,128]{2,1,0:T(8,128)(2,1)S(1)} %collective-permute-done.2.j_lo, ...), custom_call_target="tpu_custom_call" | custom-call | flops 3000000000 | bytes 6000000 | tf_op jit(solution)/shard_map/partial_gradient/pallas_call | solution.py:153
  28.4 5.1 %all-to-all-start = ((f32[8,152,128]{2,1,0:T(8,128)}), f32[8,152,128]{2,1,0:T(8,128)}, u32[]{:S(2)}, u32[]{:S(2)}) async-start(f32[8,152,128]{2,1,0:T(8,128)} %partial_gradient.2), calls=%async_computation | async-start | bytes 1245184 | tf_op jit(solution)/shard_map/all_to_all | solution.py:206
  33.5 0.1 fusion.3
  33.6 1.1 %fusion.2 = f32[2,9,16,128]{3,2,1,0:T(8,128)S(1)} fusion(f32[2,9,16,128]{3,2,1,0:T(8,128)} %param.13, f32[1,9,16,128]{3,2,1,0:T(8,128)S(1)} %get-tuple-element.26, f32[1,9,16,128]{3,2,1,0:T(8,128)S(1)} %get-tuple-element.25, f32[]{:T(128)S(6)} %copy.17, f32[]{:T(128)S(6)} %neg.3, f32[]{:T(128)S(6)} %copy.18), kind=kLoop, calls=%fused_computation.3 | loop fusion | flops 184320 | bytes 442380 | tf_op jit(solution)/shard_map/jit(clip)/min | solution.py:200
  34.7 0.0 copy-start.13
  34.8 0.7 copy-done.13
  35.4 0.0 copy-start.14
  35.4 0.6 copy-done.15
  36.1 2.6 %collective-permute-start.6 = (f32[9,1,128]{2,1,0:T(1,128)S(1)}, f32[9,1,128]{2,1,0:T(1,128)S(1)}, u32[]{:S(2)}, u32[]{:S(2)}) collective-permute-start(f32[9,1,128]{2,1,0:T(1,128)S(1)} %slice.98), channel_id=1, source_target_pairs={{0,8},{8,16},{16,24},{24,32},{32,40},{40,48},{48,56},{56,64},{64,7... | collective-permute-start | bytes 13832 | tf_op jit(solution)/shard_map/ppermute | solution.py:26
  39.3 0.7 slice.101
  40.1 2.0 %all-to-all-done = f32[8,152,128]{2,1,0:T(8,128)} async-done(((f32[8,152,128]{2,1,0:T(8,128)}), f32[8,152,128]{2,1,0:T(8,128)}, u32[]{:S(2)}, u32[]{:S(2)}) %all-to-all-start) | async-done | bytes 622624 | tf_op jit(solution)/shard_map/all_to_all | solution.py:206
  42.1 1.7 %reduce_sum.27 = f32[152,128]{1,0:T(8,128)} reduce(f32[8,152,128]{2,1,0:T(8,128)} %all-to-all-done, f32[]{:T(128)} %constant.34.clone.1), dimensions={0}, to_apply=%region_0.1 | reduce | flops 136192 | bytes 700420 | tf_op jit(solution)/shard_map/reduce_sum | solution.py:206
  43.9 0.7 slice.103
  44.5 2.9 %collective-permute-start.10 = (f32[8,128]{1,0:T(8,128)S(1)}, f32[8,128]{1,0:T(8,128)S(1)}, u32[]{:S(2)}, u32[]{:S(2)}) collective-permute-start(f32[8,128]{1,0:T(8,128)S(1)} %slice.103), channel_id=1, source_target_pairs={{8,0},{41,1},{74,2},{107,3},{140,4},{173,5},{206,6},{239,7},{16,8}... | collective-permute-start | bytes 12296 | tf_op jit(solution)/shard_map/ppermute | solution.py:214
  47.5 5.5 %collective-permute-start.11 = (f32[8,128]{1,0:T(8,128)S(1)}, f32[8,128]{1,0:T(8,128)S(1)}, u32[]{:S(2)}, u32[]{:S(2)}) collective-permute-start(f32[8,128]{1,0:T(8,128)S(1)} %slice.103), channel_id=1, source_target_pairs={{16,0},{49,1},{82,2},{115,3},{148,4},{181,5},{214,6},{247,7},{24,8... | collective-permute-start | bytes 12296 | tf_op jit(solution)/shard_map/ppermute | solution.py:214
  53.0 5.6 %collective-permute-start.12 = (f32[8,128]{1,0:T(8,128)S(1)}, f32[8,128]{1,0:T(8,128)S(1)}, u32[]{:S(2)}, u32[]{:S(2)}) collective-permute-start(f32[8,128]{1,0:T(8,128)S(1)} %slice.103), channel_id=1, source_target_pairs={{24,0},{57,1},{90,2},{123,3},{156,4},{189,5},{222,6},{255,7},{32,8... | collective-permute-start | bytes 12296 | tf_op jit(solution)/shard_map/ppermute | solution.py:214
  58.6 0.6 collective-permute-start.9
  59.2 0.9 slice.95
  60.1 1.7 %multiply_subtract_fusion.1 = (f32[9,16,128]{2,1,0:T(8,128)S(1)}, f32[9,16,128]{2,1,0:T(8,128)}) fusion(f32[9,16,128]{2,1,0:T(8,128)S(1)} %copy-done, f32[9,16,128]{2,1,0:T(8,128)S(1)} %bitcast.42, f32[]{:T(128)S(6)} %copy.16, f32[9,16,127]{2,1,0:T(8,128)} %bitcast.40, f32[9,16,1]{2,1,0:T(8,128)} %slice.101, f32[2,9,16,128]{3,2,1,0:T(8,128)} %copy-done.13, ...), kind=kLoop, calls=%fused_computation.14 | loop fusion | flops 147456 | bytes 589828 | tf_op jit(solution)/shard_map/sub | solution.py:207
  61.9 0.8 collective-permute-start.7
  62.7 0.0 collective-permute-start.8
  62.8 1.4 %collective-permute-done.7.x_lo = f32[9,16,128]{2,1,0:T(8,128)S(1)} collective-permute-done((f32[9,16,128]{2,1,0:T(8,128)S(1)}, f32[9,16,128]{2,1,0:T(8,128)S(1)}, u32[]{:S(2)}, u32[]{:S(2)}) %collective-permute-start.7) | collective-permute-done | bytes 73760 | tf_op jit(solution)/shard_map/ppermute | solution.py:26
  64.1 2.4 %collective-permute-done.8.x_hi = f32[9,16,128]{2,1,0:T(8,128)S(1)} collective-permute-done((f32[9,16,128]{2,1,0:T(8,128)S(1)}, f32[9,16,128]{2,1,0:T(8,128)S(1)}, u32[]{:S(2)}, u32[]{:S(2)}) %collective-permute-start.8) | collective-permute-done | bytes 73760 | tf_op jit(solution)/shard_map/ppermute | solution.py:26
  66.5 0.9 copy-done.7
  67.5 0.9 copy-done.10
  68.4 0.9 copy-done.12
  69.3 6.8 %partial_gradient.3 = f32[8,152,128]{2,1,0:T(8,128)S(1)} custom-call(f32[1]{0:T(128)} %bitcast.31.clip_ref, f32[9,16,128]{2,1,0:T(8,128)S(1)} %collective-permute-done.7.x_lo, f32[9,16,128]{2,1,0:T(8,128)S(1)} %get-tuple-element.19.x_own, f32[9,16,128]{2,1,0:T(8,128)S(1)} %collective-permute-done.8.x_hi, bf16[36,16,128]{2,1,0:T(8,128)(2,1)S(1)} %copy-done.10, ...), custom_call_target="tpu_custom_call" | custom-call | flops 3000000000 | bytes 6000000 | tf_op jit(solution)/shard_map/partial_gradient/pallas_call | solution.py:153
  76.1 24.2 %all_to_all.10 = f32[8,152,128]{2,1,0:T(8,128)S(1)} all-to-all(f32[8,152,128]{2,1,0:T(8,128)S(1)} %broadcast_dynamic-update-slice_fusion), channel_id=1, replica_groups=mesh['tile_0'=2,'tile_1'=8,'tile_2'=2,'wave_0'=2,'wave_1'=4] {'wave_0','..., dimensions={0} | all-to-all | bytes 1245184 | tf_op jit(solution)/shard_map/all_to_all | solution.py:228
  100.3 0.6 slice_reduce_fusion
  100.9 0.6 multiply_subtract_fusion
  (51 shorter events, 0.2 us)
Async XLA Ops:
  0.6 17.4 %copy-start.8 = (bf16[4,9,16,128]{3,2,1,0:T(8,128)(2,1)S(1)}, bf16[4,9,16,128]{3,2,1,0:T(8,128)(2,1)}, u32[]{:S(2)}) copy-start(bf16[4,9,16,128]{3,2,1,0:T(8,128)(2,1)} %param.14) | copy-start | bytes 442372
  0.6 17.4 %copy-start.1 = (bf16[4,32,16,128]{3,2,1,0:T(8,128)(2,1)S(1)}, bf16[4,32,16,128]{3,2,1,0:T(8,128)(2,1)}, u32[]{:S(2)}) copy-start(bf16[4,32,16,128]{3,2,1,0:T(8,128)(2,1)} %param.16) | copy-start | bytes 1572868
  0.7 6.5 %copy-start = (f32[9,16,128]{2,1,0:T(8,128)S(1)}, f32[9,16,128]{2,1,0:T(8,128)}, u32[]{:S(2)}) copy-start(f32[9,16,128]{2,1,0:T(8,128)} %x_own.1) | copy-start | bytes 221188
  0.7 6.7 %copy-start.17 = (bf16[17,17]{1,0:T(8,128)(2,1)S(1)}, bf16[17,17]{1,0:T(8,128)(2,1)}, u32[]{:S(2)}) copy-start(bf16[17,17]{1,0:T(8,128)(2,1)} %param.17) | copy-start | bytes 1738
  0.7 17.3 %collective-permute-start.2 = (bf16[36,16,128]{2,1,0:T(8,128)(2,1)}, bf16[36,16,128]{2,1,0:T(8,128)(2,1)S(1)}, u32[]{:S(2)}, u32[]{:S(2)}) collective-permute-start(bf16[36,16,128]{2,1,0:T(8,128)(2,1)} %bitcast.36), channel_id=1, source_target_pairs={{0,8},{8,16},{16,24},{24,32},{32,40},{40,48},{48,56},{56,64},{64,7... | collective-permute-start | bytes 442376 | tf_op jit(solution)/shard_map/ppermute | solution.py:26
  2.9 15.0 %collective-permute-start.3 = (bf16[36,16,128]{2,1,0:T(8,128)(2,1)}, bf16[36,16,128]{2,1,0:T(8,128)(2,1)S(1)}, u32[]{:S(2)}, u32[]{:S(2)}) collective-permute-start(bf16[36,16,128]{2,1,0:T(8,128)(2,1)} %bitcast.37), channel_id=1, source_target_pairs={{0,248},{8,0},{16,8},{24,16},{32,24},{40,32},{48,40},{56,48},{64,5... | collective-permute-start | bytes 442376 | tf_op jit(solution)/shard_map/ppermute | solution.py:26
  4.0 14.0 %collective-permute-start.4 = (bf16[128,8,128]{2,1,0:T(8,128)(2,1)S(1)}, bf16[128,8,128]{2,1,0:T(8,128)(2,1)S(1)}, u32[]{:S(2)}, u32[]{:S(2)}) collective-permute-start(bf16[128,8,128]{2,1,0:T(8,128)(2,1)S(1)} %get-tuple-element.22), channel_id=1, source_target_pairs={{0,8},{8,16},{16,24},{24,32},{32,40},{40,48},{48,56},{56,64},{64,7... | collective-permute-start | bytes 786440 | tf_op jit(solution)/shard_map/ppermute | solution.py:26
  5.8 12.2 %collective-permute-start.5 = (bf16[128,8,128]{2,1,0:T(8,128)(2,1)S(1)}, bf16[128,8,128]{2,1,0:T(8,128)(2,1)S(1)}, u32[]{:S(2)}, u32[]{:S(2)}) collective-permute-start(bf16[128,8,128]{2,1,0:T(8,128)(2,1)S(1)} %get-tuple-element.21), channel_id=1, source_target_pairs={{0,248},{8,0},{16,8},{24,16},{32,24},{40,32},{48,40},{56,48},{64,5... | collective-permute-start | bytes 786440 | tf_op jit(solution)/shard_map/ppermute | solution.py:26
  5.8 8.9 %collective-permute-start.1 = (f32[9,16,128]{2,1,0:T(8,128)}, f32[9,16,128]{2,1,0:T(8,128)S(1)}, u32[]{:S(2)}, u32[]{:S(2)}) collective-permute-start(f32[9,16,128]{2,1,0:T(8,128)} %x_own.1), channel_id=1, source_target_pairs={{0,248},{8,0},{16,8},{24,16},{32,24},{40,32},{48,40},{56,48},{64,5... | collective-permute-start | bytes 221192 | tf_op jit(solution)/shard_map/ppermute | solution.py:26
  14.8 3.2 %collective-permute-start = (f32[9,16,128]{2,1,0:T(8,128)S(1)}, f32[9,16,128]{2,1,0:T(8,128)S(1)}, u32[]{:S(2)}, u32[]{:S(2)}) collective-permute-start(f32[9,16,128]{2,1,0:T(8,128)S(1)} %copy-done), channel_id=1, source_target_pairs={{0,8},{8,16},{16,24},{24,32},{32,40},{40,48},{48,56},{56,64},{64,7... | collective-permute-start | bytes 221192 | tf_op jit(solution)/shard_map/ppermute | solution.py:26
  18.0 10.4 %copy-start.9 = (bf16[36,16,128]{2,1,0:T(8,128)(2,1)}, bf16[36,16,128]{2,1,0:T(8,128)(2,1)S(1)}, u32[]{:S(2)}) copy-start(bf16[36,16,128]{2,1,0:T(8,128)(2,1)S(1)} %collective-permute-done.2.j_lo) | copy-start | bytes 442372
  18.0 10.4 %copy-start.11 = (bf16[36,16,128]{2,1,0:T(8,128)(2,1)}, bf16[36,16,128]{2,1,0:T(8,128)(2,1)S(1)}, u32[]{:S(2)}) copy-start(bf16[36,16,128]{2,1,0:T(8,128)(2,1)S(1)} %collective-permute-done.3.j_hi) | copy-start | bytes 442372
  18.0 10.4 %copy-start.6 = (bf16[128,8,128]{2,1,0:T(8,128)(2,1)}, bf16[128,8,128]{2,1,0:T(8,128)(2,1)S(1)}, u32[]{:S(2)}) copy-start(bf16[128,8,128]{2,1,0:T(8,128)(2,1)S(1)} %collective-permute-done.5.o_hi) | copy-start | bytes 786436
  18.0 1.4 %copy-start.2 = (bf16[2304,256]{1,0:T(8,128)(2,1)S(1)}, bf16[2304,256]{1,0:T(8,128)(2,1)}, u32[]{:S(2)}) copy-start(bf16[2304,256]{1,0:T(8,128)(2,1)} %get-tuple-element.17.forward_ref) | copy-start | bytes 3538948
  19.5 1.3 %copy-start.4 = (bf16[2304,256]{1,0:T(8,128)(2,1)S(1)}, bf16[2304,256]{1,0:T(8,128)(2,1)}, u32[]{:S(2)}) copy-start(bf16[2304,256]{1,0:T(8,128)(2,1)} %get-tuple-element.18.adjoint_ref) | copy-start | bytes 3538948
  28.4 13.7 %all-to-all-start = ((f32[8,152,128]{2,1,0:T(8,128)}), f32[8,152,128]{2,1,0:T(8,128)}, u32[]{:S(2)}, u32[]{:S(2)}) async-start(f32[8,152,128]{2,1,0:T(8,128)} %partial_gradient.2), calls=%async_computation | async-start | bytes 1245184 | tf_op jit(solution)/shard_map/all_to_all | solution.py:206
  33.6 32.9 %copy-start.3 = (bf16[2304,256]{1,0:T(8,128)(2,1)S(1)}, bf16[2304,256]{1,0:T(8,128)(2,1)}, u32[]{:S(2)}) copy-start(bf16[2304,256]{1,0:T(8,128)(2,1)} %get-tuple-element.17.forward_ref) | copy-start | bytes 3538948
  33.6 32.9 %copy-start.5 = (bf16[2304,256]{1,0:T(8,128)(2,1)S(1)}, bf16[2304,256]{1,0:T(8,128)(2,1)}, u32[]{:S(2)}) copy-start(bf16[2304,256]{1,0:T(8,128)(2,1)} %get-tuple-element.18.adjoint_ref) | copy-start | bytes 3538948
  34.7 0.7 copy-start.13
  35.4 0.6 copy-start.15
  35.4 24.7 %copy-start.14 = (f32[9,16,128]{2,1,0:T(8,128)}, f32[9,16,128]{2,1,0:T(8,128)S(1)}, u32[]{:S(2)}) copy-start(f32[9,16,128]{2,1,0:T(8,128)S(1)} %get-tuple-element.24) | copy-start | bytes 221188
  36.1 24.1 %collective-permute-start.6 = (f32[9,1,128]{2,1,0:T(1,128)S(1)}, f32[9,1,128]{2,1,0:T(1,128)S(1)}, u32[]{:S(2)}, u32[]{:S(2)}) collective-permute-start(f32[9,1,128]{2,1,0:T(1,128)S(1)} %slice.98), channel_id=1, source_target_pairs={{0,8},{8,16},{16,24},{24,32},{32,40},{40,48},{48,56},{56,64},{64,7... | collective-permute-start | bytes 13832 | tf_op jit(solution)/shard_map/ppermute | solution.py:26
  44.5 18.2 %collective-permute-start.10 = (f32[8,128]{1,0:T(8,128)S(1)}, f32[8,128]{1,0:T(8,128)S(1)}, u32[]{:S(2)}, u32[]{:S(2)}) collective-permute-start(f32[8,128]{1,0:T(8,128)S(1)} %slice.103), channel_id=1, source_target_pairs={{8,0},{41,1},{74,2},{107,3},{140,4},{173,5},{206,6},{239,7},{16,8}... | collective-permute-start | bytes 12296 | tf_op jit(solution)/shard_map/ppermute | solution.py:214
  47.5 15.3 %collective-permute-start.11 = (f32[8,128]{1,0:T(8,128)S(1)}, f32[8,128]{1,0:T(8,128)S(1)}, u32[]{:S(2)}, u32[]{:S(2)}) collective-permute-start(f32[8,128]{1,0:T(8,128)S(1)} %slice.103), channel_id=1, source_target_pairs={{16,0},{49,1},{82,2},{115,3},{148,4},{181,5},{214,6},{247,7},{24,8... | collective-permute-start | bytes 12296 | tf_op jit(solution)/shard_map/ppermute | solution.py:214
  53.0 9.8 %collective-permute-start.12 = (f32[8,128]{1,0:T(8,128)S(1)}, f32[8,128]{1,0:T(8,128)S(1)}, u32[]{:S(2)}, u32[]{:S(2)}) collective-permute-start(f32[8,128]{1,0:T(8,128)S(1)} %slice.103), channel_id=1, source_target_pairs={{24,0},{57,1},{90,2},{123,3},{156,4},{189,5},{222,6},{255,7},{32,8... | collective-permute-start | bytes 12296 | tf_op jit(solution)/shard_map/ppermute | solution.py:214
  58.6 4.2 %collective-permute-start.9 = (f32[8,128]{1,0:T(8,128)S(1)}, f32[8,128]{1,0:T(8,128)S(1)}, u32[]{:S(2)}, u32[]{:S(2)}) collective-permute-start(f32[8,128]{1,0:T(8,128)S(1)} %slice.103), channel_id=1, source_target_pairs={{0,0},{33,1},{66,2},{99,3},{132,4},{165,5},{198,6},{231,7},{8,8},{... | collective-permute-start | bytes 12296 | tf_op jit(solution)/shard_map/ppermute | solution.py:214
  61.9 2.2 %collective-permute-start.7 = (f32[9,16,128]{2,1,0:T(8,128)S(1)}, f32[9,16,128]{2,1,0:T(8,128)S(1)}, u32[]{:S(2)}, u32[]{:S(2)}) collective-permute-start(f32[9,16,128]{2,1,0:T(8,128)S(1)} %get-tuple-element.19.x_own), channel_id=1, source_target_pairs={{0,8},{8,16},{16,24},{24,32},{32,40},{40,48},{48,56},{56,64},{64,7... | collective-permute-start | bytes 221192 | tf_op jit(solution)/shard_map/ppermute | solution.py:26
  62.7 3.8 %collective-permute-start.8 = (f32[9,16,128]{2,1,0:T(8,128)S(1)}, f32[9,16,128]{2,1,0:T(8,128)S(1)}, u32[]{:S(2)}, u32[]{:S(2)}) collective-permute-start(f32[9,16,128]{2,1,0:T(8,128)S(1)} %get-tuple-element.19.x_own), channel_id=1, source_target_pairs={{0,248},{8,0},{16,8},{24,16},{32,24},{40,32},{48,40},{56,48},{64,5... | collective-permute-start | bytes 221192 | tf_op jit(solution)/shard_map/ppermute | solution.py:26
  66.5 1.0 copy-start.7
  67.5 0.9 copy-start.10
  68.4 0.9 copy-start.12
  76.1 24.8 %copy-start.16 = (f32[9,16,128]{2,1,0:T(8,128)S(1)}, f32[9,16,128]{2,1,0:T(8,128)}, u32[]{:S(2)}) copy-start(f32[9,16,128]{2,1,0:T(8,128)} %get-tuple-element.20) | copy-start | bytes 221188

commit v2 on v1

v2 whole, which is shorter than its diff:
```python
import functools

import jax
import jax.numpy as jnp
from jax import lax
from jax.experimental import pallas as pl
from jax.experimental.pallas import tpu as pltpu
from jax.sharding import Mesh
from jax.sharding import PartitionSpec as P

TILE = ("tile_0", "tile_1", "tile_2")
WAVE = ("wave_0", "wave_1")
ALL = TILE + WAVE
F32 = jnp.float32
BF16 = jnp.bfloat16

SP = 36
SPP = 40
HL = 2 * SPP
TAPS = 17
PAIRS = 9
LANES = 128
AT_JAC = 1024
AT_X = AT_JAC + SP * 16
AT_DUAL = AT_X + 3 * 144
HALO = AT_DUAL + 48


def neighbours(tiles, waves, by):
    return [
        (t * waves + w, ((t + by) % tiles) * waves + w) for t in range(tiles) for w in range(waves)
    ]


def passed_along(x, by):
    return lax.ppermute(x, ALL, neighbours(lax.axis_size(TILE), lax.axis_size(WAVE), by))


def rounded(value):
    return value.astype(BF16).astype(F32)


def split_rows(value):
    high = rounded(value)
    return jnp.concatenate([high, value - high], axis=0).astype(BF16)


def thirds(value):
    high = rounded(value)
    mid = rounded(value - high)
    return high, mid, value - high - mid


def halo_kernel(x_ref, dual_ref, jac_ref, obs_ref, up_ref, down_ref):
    dual = jnp.concatenate([dual_ref[0, :, 15, :], jnp.zeros((7, LANES), F32)], axis=0)
    duals = thirds(dual)
    for ref, first in ((up_ref, 8), (down_ref, 0)):
        ref[0:AT_JAC, :] = obs_ref[:, first : first + 8, :].reshape(AT_JAC, LANES)
        ref[AT_JAC:AT_X, :] = jac_ref[...].reshape(SP * 16, LANES)
        for i in range(3):
            ref[AT_DUAL + 16 * i : AT_DUAL + 16 * i + 16, :] = duals[i].astype(BF16)
    for p in range(9):
        for i, part in enumerate(thirds(x_ref[p])):
            at = AT_X + 144 * i + 16 * p
            up_ref[at : at + 16, :] = part.astype(BF16)
            down_ref[at : at + 16, :] = part.astype(BF16)


def halo_x(ref, p):
    return sum(ref[AT_X + 144 * i + 16 * p : AT_X + 144 * i + 16 * p + 16, :].astype(F32) for i in range(3))


def weights_kernel(psf_ref, obs_ref, forward_ref, adjoint_ref, seen_ref, rows_ref):
    n = LANES
    row = lax.broadcasted_iota(jnp.int32, (n, n), 0)
    col = lax.broadcasted_iota(jnp.int32, (n, n), 1)
    offset = lax.rem(row - col + (n + 8), n)
    zero = jnp.zeros((n, n), BF16)
    for ref in (forward_ref, adjoint_ref):
        ref[0:n, n : 2 * n] = zero
        ref[TAPS * n : (TAPS + 1) * n, 0:n] = zero
    for tap in range(TAPS):
        for ref, flip in ((forward_ref, False), (adjoint_ref, True)):
            mat = jnp.zeros((n, n), F32)
            for b in range(TAPS):
                scalar = psf_ref[16 - tap, 16 - b] if flip else psf_ref[tap, b]
                mat = jnp.where(offset == b, scalar, mat)
            mat = mat.astype(BF16)
            ref[tap * n : (tap + 1) * n, 0:n] = mat
            ref[(tap + 1) * n : (tap + 2) * n, n : 2 * n] = mat
    rows_ref[...] = obs_ref[...].astype(F32).reshape(128 * 16, n)
    for r in range(16):
        seen_ref[:, r * n : (r + 1) * n] = rows_ref[pl.ds(r, 128, stride=16), :]


def step_kernel(
    first,
    clip_ref,
    lo_ref, hi_ref, x_lo, x_own, x_hi, jac_ref, seen_ref,
    resp_ref, resp_t_ref, forward_ref, adjoint_ref,
    out_ref,
    terms, stacked, halo, contracted, along,
):
    n = LANES
    clip = clip_ref[0]
    terms[SP * 48 : SPP * 48, :] = jnp.zeros(((SPP - SP) * 48, n), F32)
    for part, (x_ref, ref) in enumerate(((x_lo, lo_ref), (x_own, None), (x_hi, hi_ref))):
        for p in range(9):
            if first and ref is not None:
                x = halo_x(ref, p)
            else:
                x = x_ref[p * 16 : p * 16 + 16, :]
            for s in range(4):
                image = s * 9 + p
                if ref is None:
                    jac = jac_ref[image]
                else:
                    jac = ref[AT_JAC + image * 16 : AT_JAC + image * 16 + 16, :]
                terms[image * 48 + part * 16 : image * 48 + part * 16 + 16, :] = (
                    jac.astype(F32) * x
                )
    halo[0:AT_JAC, :] = lo_ref[0:AT_JAC, :].astype(F32)
    halo[AT_JAC : 2 * AT_JAC, :] = hi_ref[0:AT_JAC, :].astype(F32)
    for row in range(48):
        pair, half = row // 2, row % 2
        stacked[pair * HL : (pair + 1) * HL, half * n : (half + 1) * n] = split_rows(
            terms[pl.ds(row, SPP, stride=48), :]
        )
    huber = jnp.zeros((8, 8 * n), F32)
    for block in range(4):
        windows = [
            stacked[(4 * block + k) * HL : (4 * block + k + 4) * HL, :] for k in range(PAIRS)
        ]
        blurred = jnp.dot(
            jnp.concatenate(windows, axis=1), forward_ref[...], preferred_element_type=F32
        )
        model = jnp.concatenate(
            [
                blurred[i * HL : i * HL + SPP] + blurred[i * HL + SPP : (i + 1) * HL]
                for i in range(4)
            ],
            axis=1,
        )
        high = rounded(model)
        model = jnp.concatenate(
            [high, model - high, high, jnp.zeros((8, 8 * n), F32)], axis=0
        ).astype(BF16)
        if block in (1, 2):
            seen = seen_ref[:, (block - 1) * 8 * n : block * 8 * n]
        else:
            at = 0 if block == 0 else AT_JAC
            seen = jnp.concatenate(
                [halo[pl.ds(at + r, 128, stride=8), :] for r in range(8)], axis=1
            )
        resid = jnp.dot(resp_ref[...], model, preferred_element_type=F32) - seen
        weighted = jnp.clip(resid, -clip, clip)
        if first and block in (1, 2):
            loss = weighted * (resid - 0.5 * weighted)
            huber = huber + jnp.sum(loss.reshape(16, 8, 8 * n), axis=0)
        summed = jnp.dot(resp_t_ref[...], weighted.astype(BF16), preferred_element_type=F32)
        summed = split_rows(summed[:SPP] + summed[SPP:])
        for i in range(4):
            pair = 4 * block + i
            contracted[pair * HL : (pair + 1) * HL, :] = summed[:, 2 * n * i : 2 * n * (i + 1)]
    for block in range(2):
        windows = [
            contracted[(4 * block + k) * HL : (4 * block + k + 4) * HL, :] for k in range(PAIRS)
        ]
        back = jnp.dot(
            jnp.concatenate(windows, axis=1), adjoint_ref[...], preferred_element_type=F32
        )
        for i in range(4):
            pair = 4 * block + i
            both = back[i * HL : i * HL + SPP] + back[i * HL + SPP : (i + 1) * HL]
            along[pl.ds(2 * pair, SPP, stride=16), :] = both[:, :n]
            along[pl.ds(2 * pair + 1, SPP, stride=16), :] = both[:, n:]
    for p in range(9):
        total = jnp.zeros((16, n), F32)
        for s in range(4):
            image = s * 9 + p
            total = total + jac_ref[image].astype(F32) * along[image * 16 : image * 16 + 16, :]
        for copy in range(8):
            out_ref[copy, p * 16 : p * 16 + 16, :] = total
    loss = sum(huber[:, i * n : (i + 1) * n] for i in range(8))
    for copy in range(8):
        out_ref[copy, 144:152, :] = loss


def dual_kernel(step_ref, dual_step_ref, bound_ref, x_ref, dual_ref, lo_ref, hi_ref, dual_out_ref, moved_ref):
    n = LANES
    bound, dual_step = bound_ref[0], dual_step_ref[0]
    row = lax.broadcasted_iota(jnp.int32, (16, n), 0)
    duals = sum(lo_ref[AT_DUAL + 16 * i : AT_DUAL + 16 * i + 16, :].astype(F32) for i in range(3))
    for p in range(9):
        x = x_ref[p]
        after = halo_x(hi_ref, p)[0:1]
        before = halo_x(lo_ref, p)[15:16]
        grad_r = jnp.where(row == 15, after, pltpu.roll(x, 15, 0)) - x
        grad_c = pltpu.roll(x, n - 1, 1) - x
        dual_r = jnp.clip(dual_ref[0, p] + dual_step * grad_r, -bound, bound)
        dual_c = jnp.clip(dual_ref[1, p] + dual_step * grad_c, -bound, bound)
        prior = jnp.clip(duals[p : p + 1] + dual_step * (x[0:1] - before), -bound, bound)
        divergence = dual_r - jnp.where(row == 0, prior, pltpu.roll(dual_r, 1, 0))
        divergence = divergence + (dual_c - pltpu.roll(dual_c, 1, 1))
        dual_out_ref[0, p] = dual_r
        dual_out_ref[1, p] = dual_c
        moved_ref[p * 16 : p * 16 + 16, :] = step_ref[0] * divergence


def update_kernel(step_ref, whole_ref, x_ref, moved_ref, out_ref):
    total = sum(whole_ref[i] for i in range(8))
    out_ref[0:144, :] = x_ref[0:144, :] + moved_ref[...] - step_ref[0] * total[:144]
    out_ref[144:152, :] = total[144:]


def vmem_specs(count):
    return [pl.BlockSpec(memory_space=pltpu.VMEM) for _ in range(count)]


def smem_specs(count):
    return [pl.BlockSpec(memory_space=pltpu.SMEM) for _ in range(count)]


def call(kernel, shapes, scalars, arrays, name, scratch=(), flops=0):
    single = not isinstance(shapes, tuple)
    moved = sum(a.size * a.dtype.itemsize for a in arrays)
    return pl.pallas_call(
        kernel,
        out_shape=shapes,
        in_specs=smem_specs(len(scalars)) + vmem_specs(len(arrays)),
        out_specs=vmem_specs(1)[0] if single else tuple(vmem_specs(len(shapes))),
        scratch_shapes=list(scratch),
        compiler_params=pltpu.CompilerParams(vmem_limit_bytes=40 * 1024 * 1024),
        cost_estimate=pl.CostEstimate(flops=flops, bytes_accessed=moved, transcendentals=0),
        name=name,
    )(*[s.reshape(1) if s.ndim == 0 else s for s in scalars], *arrays)


def shaped(shape, dtype):
    return jax.ShapeDtypeStruct(shape, dtype)


def partial_gradient(first, clip_bound, halos, xs, jac, seen, resp, resp_t, forward, adjoint):
    return call(
        functools.partial(step_kernel, first),
        shaped((8, 152, LANES), F32),
        (clip_bound,),
        (*halos, *xs, jac, seen, resp, resp_t, forward, adjoint),
        "partial_gradient",
        (
            pltpu.VMEM((SPP * 48, LANES), F32),
            pltpu.VMEM((24 * HL, 2 * LANES), BF16),
            pltpu.VMEM((2 * AT_JAC, LANES), F32),
            pltpu.VMEM((16 * HL, 2 * LANES), BF16),
            pltpu.VMEM((SPP * 16, LANES), F32),
        ),
        flops=3_000_000_000,
    )


def response_matrices(response):
    block = jnp.einsum("st,pl->sltp", jnp.eye(4, dtype=F32), response).reshape(128, SP)
    block = jnp.pad(block, ((0, 0), (0, SPP - SP)))
    high = lax.reduce_precision(block, 8, 7)
    low = block - high
    forward = jnp.concatenate([high, high, low, jnp.zeros((128, 8), F32)], axis=1)
    backward = jnp.concatenate([high.T, low.T], axis=0)
    return forward.astype(BF16), backward.astype(BF16)


def per_device(
    params, dual_in, jacobian, response, observed, psf, step_size, dual_step, tv_bound, clip_bound
):
    stokes, waves, rows, ncol = observed.shape
    tiles, wavs = lax.axis_size(TILE), lax.axis_size(WAVE)
    jac = jacobian.reshape(SP, rows, ncol)
    obs = observed.reshape(stokes * waves, rows, ncol)
    flat = params.reshape(9 * rows, ncol)
    buffer = shaped((HALO, LANES), BF16)
    up, down = call(halo_kernel, (buffer, buffer), (), (params, dual_in, jac, obs), "halos")
    halos = (passed_along(up, 1), passed_along(down, -1))
    weights = shaped((18 * LANES, 2 * LANES), BF16)
    forward, adjoint, seen = call(
        weights_kernel,
        (weights, weights, shaped((stokes * waves, rows * ncol), F32)),
        (psf.astype(F32),),
        (obs,),
        "weights",
        (pltpu.VMEM((128 * 16, LANES), F32),),
        flops=5_000_000_000,
    )
    resp, resp_t = response_matrices(response)
    gradient = functools.partial(
        partial_gradient,
        clip_bound=clip_bound, halos=halos, jac=jac, seen=seen,
        resp=resp, resp_t=resp_t, forward=forward, adjoint=adjoint,
    )
    part = gradient(True, xs=(flat, flat, flat))
    whole = lax.all_to_all(part, WAVE, 0, 0, tiled=True)
    dual_out, moved = call(
        dual_kernel,
        (shaped((2, 9, rows, ncol), F32), shaped((9 * rows, ncol), F32)),
        (step_size, dual_step, tv_bound),
        (params, dual_in, *halos),
        "dual",
        flops=20_000_000,
    )
    updated = shaped((9 * rows + 8, ncol), F32)
    state = call(update_kernel, updated, (step_size,), (whole, flat, moved), "update")
    before, after = passed_along(state, 1), passed_along(state, -1)
    second = passed_along(state[9 * rows :], -2)
    loss = before[9 * rows :] + state[9 * rows :] + after[9 * rows :] + second
    each = tiles // wavs
    loss = lax.ppermute(
        loss,
        ALL,
        [
            (((t + each * w + 2) % tiles) * wavs + w, t * wavs + w)
            for t in range(tiles)
            for w in range(wavs)
        ],
    )
    part = gradient(False, xs=(before, state, after))
    part = part.at[:, 9 * rows :].set(loss)
    whole = lax.all_to_all(part, WAVE, 0, 0, tiled=True)
    state = call(update_kernel, updated, (step_size,), (whole, state, moved), "update")
    total = stokes * waves * wavs * rows * tiles * ncol
    misfit = jnp.sum(state[9 * rows :]) / total
    return (state[: 9 * rows].reshape(9, rows, ncol), dual_out, misfit)


def solution(mesh):
    split = Mesh(
        mesh.devices.reshape(2, 8, 2, 2, 4), ("tile_0", "tile_1", "tile_2", "wave_0", "wave_1")
    )
    placed = (
        P(None, TILE, None),
        P(None, None, TILE, None),
        P(None, None, TILE, None),
        P(None, WAVE),
        P(None, WAVE, TILE, None),
        P(),
        P(),
        P(),
        P(),
        P(),
    )
    return jax.shard_map(
        per_device,
        mesh=split,
        in_specs=placed,
        out_specs=(P(None, TILE, None), P(None, None, TILE, None), P()),
        check_vma=False,
    )
```

time: 104 us -> 79.7 us (0.77)
  the two profiles are of different devices: /device:TPU:65 before, /device:TPU:2 now
where the time goes in v2:
time: 79.7 us; the launch traced here: 79.2 us
  starting transfers between devices  22.5 us (28%)
  Pallas kernels  16.1 us (20%)
  blocking collectives  14.8 us (19%)
  local copies, waits for them, and re-layouts  10.2 us (13%)
  waiting for transfers between devices  8.86 us (11%)
  between operations  5.28 us (7%)
  other arithmetic  1.48 us (2%)
    pallas_call x7, Pallas kernels, call(): pl.pallas_call(kernel, out_shape=shapes, in_specs=smem_specs(len(scalars)...  16.1 us
    all_to_all x1, blocking collectives, per_device(): whole = lax.all_to_all(part, WAVE, 0, 0, tiled=True)  14.8 us
    ppermute x5, starting transfers between devices, passed_along(): lax.ppermute(x, ALL, neighbours(lax.axis_size(TILE), lax.axis_size(WAVE),...  13.3 us
    unnamed x30, local copies, waits for them, and re-layouts  9.28 us
    all_to_all x1, starting transfers between devices, per_device(): whole = lax.all_to_all(part, WAVE, 0, 0, tiled=True)  6.05 us
    all_to_all x1, waiting for transfers between devices, per_device(): whole = lax.all_to_all(part, WAVE, 0, 0, tiled=True)  4.94 us
    ppermute x5, waiting for transfers between devices, passed_along(): lax.ppermute(x, ALL, neighbours(lax.axis_size(TILE), lax.axis_size(WAVE),...  3.92 us
    ppermute x1, starting transfers between devices, per_device(): lax.ppermute(loss, ALL, [((t + each * w + 2) % tiles * wavs + w, t * wavs...  3.16 us
  transfers between devices with their start and end apart: 7, of which 3 were waited for; matrix products, arithmetic and copies ran while one was open for 1% of the time, Pallas kernels for 12%

profile of v2, /device:TPU:2, one launch (start us, length us, event | category | flops | bytes accessed | tf_op | source)
XLA Modules:
  0.0 79.2 jit_solution(6146022147891534765)
XLA Ops:
  0.6 0.0 copy-start
  0.6 0.9 %copy-done = f32[9,16,128]{2,1,0:T(8,128)S(1)} copy-done((f32[9,16,128]{2,1,0:T(8,128)S(1)}, f32[9,16,128]{2,1,0:T(8,128)}, u32[]{:S(2)}) %copy-start) | copy-done | bytes 73752
  1.5 0.0 copy-start.2
  1.5 0.9 %copy-done.2 = f32[2,9,16,128]{3,2,1,0:T(8,128)S(1)} copy-done((f32[2,9,16,128]{3,2,1,0:T(8,128)S(1)}, f32[2,9,16,128]{3,2,1,0:T(8,128)}, u32[]{:S(2)}) %copy-start.2) | copy-done | bytes 147480
  2.4 1.0 %copy-done.4 = bf16[4,32,16,128]{3,2,1,0:T(8,128)(2,1)S(1)} copy-done((bf16[4,32,16,128]{3,2,1,0:T(8,128)(2,1)S(1)}, bf16[4,32,16,128]{3,2,1,0:T(8,128)(2,1)}, u32[]{:S(2)}) %copy-start.4) | copy-done | bytes 524312
  3.5 0.0 copy-start.6
  3.5 0.9 %copy-done.6 = bf16[4,9,16,128]{3,2,1,0:T(8,128)(2,1)S(1)} copy-done((bf16[4,9,16,128]{3,2,1,0:T(8,128)(2,1)S(1)}, bf16[4,9,16,128]{3,2,1,0:T(8,128)(2,1)}, u32[]{:S(2)}) %copy-start.6) | copy-done | bytes 147480
  4.4 0.1 halos.1
  4.5 0.1 collective-permute-start
  4.6 6.9 %collective-permute-start.1 = (bf16[2080,128]{1,0:T(8,128)(2,1)S(1)}, bf16[2080,128]{1,0:T(8,128)(2,1)S(1)}, u32[]{:S(2)}, u32[]{:S(2)}) collective-permute-start(bf16[2080,128]{1,0:T(8,128)(2,1)S(1)} %get-tuple-element.23), channel_id=1, source_target_pairs={{0,248},{1,249},{2,250},{3,251},{4,252},{5,253},{6,254},{7,255},{8... | collective-permute-start | bytes 1597448 | tf_op jit(solution)/shard_map/ppermute | solution.py:36
  11.6 0.8 multiply_bitcast_fusion
  12.3 0.1 reshape.70
  12.5 0.1 pad.12.clone
  12.6 0.1 maximum_maximum_fusion
  12.6 0.1 copy.13.resp_ref
  12.8 0.0 copy-done.14
  13.4 0.0 copy-done.5
  13.5 0.0 copy-start.1
  13.5 0.0 copy-start.7
  13.5 3.8 %weights.1 = (bf16[2304,256]{1,0:T(8,128)(2,1)S(1)}, bf16[2304,256]{1,0:T(8,128)(2,1)S(1)}, f32[128,2048]{1,0:T(8,128)S(1)}) custom-call(f32[17,17]{1,0:T(8,128)S(1)} %convert_element_type.4.psf_ref, bf16[128,16,128]{2,1,0:T(8,128)(2,1)S(1)} %bitcast.26), custom_call_target="tpu_custom_call" | custom-call | flops 5000000000 | bytes 524288 | tf_op jit(solution)/shard_map/weights/pallas_call | solution.py:227
  17.3 1.2 %collective-permute-done.lo_ref = bf16[2080,128]{1,0:T(8,128)(2,1)S(1)} collective-permute-done((bf16[2080,128]{1,0:T(8,128)(2,1)S(1)}, bf16[2080,128]{1,0:T(8,128)(2,1)S(1)}, u32[]{:S(2)}, u32[]{:S(2)}) %collective-permute-start) | collective-permute-done | bytes 532512 | tf_op jit(solution)/shard_map/ppermute | solution.py:36
  18.4 0.0 collective-permute-done.1.hi_ref
  18.4 0.0 copy-done.1
  18.4 0.0 copy-done.7
  18.4 6.0 %partial_gradient.2 = f32[8,152,128]{2,1,0:T(8,128)} custom-call(f32[1]{0:T(128)} %bitcast.19.clip_ref, bf16[2080,128]{1,0:T(8,128)(2,1)S(1)} %collective-permute-done.lo_ref, bf16[2080,128]{1,0:T(8,128)(2,1)S(1)} %collective-permute-done.1.hi_ref, f32[144,128]{1,0:T(8,128)S(1)} %bitcast.21, f32[144,128]{1,0:T(8,128)S(1)} %bitcast.22, ...), custom_call_target="tpu_custom_call" | custom-call | flops 3000000000 | bytes 4894720 | tf_op jit(solution)/shard_map/partial_gradient/pallas_call | solution.py:227
  24.5 1.0 %copy-done.8 = bf16[2304,256]{1,0:T(8,128)(2,1)} copy-done((bf16[2304,256]{1,0:T(8,128)(2,1)}, bf16[2304,256]{1,0:T(8,128)(2,1)S(1)}, u32[]{:S(2)}) %copy-start.8) | copy-done | bytes 1179672
  25.5 1.0 %copy-done.10 = bf16[2304,256]{1,0:T(8,128)(2,1)} copy-done((bf16[2304,256]{1,0:T(8,128)(2,1)}, bf16[2304,256]{1,0:T(8,128)(2,1)S(1)}, u32[]{:S(2)}) %copy-start.10) | copy-done | bytes 1179672
  26.5 1.0 %copy-done.12 = f32[128,2048]{1,0:T(8,128)} copy-done((f32[128,2048]{1,0:T(8,128)}, f32[128,2048]{1,0:T(8,128)S(1)}, u32[]{:S(2)}) %copy-start.12) | copy-done | bytes 1048600
  27.5 6.1 %all-to-all-start = ((f32[8,152,128]{2,1,0:T(8,128)}), f32[8,152,128]{2,1,0:T(8,128)S(1)}, u32[]{:S(2)}, u32[]{:S(2)}) async-start(f32[8,152,128]{2,1,0:T(8,128)} %partial_gradient.2), calls=%async_computation | async-start | bytes 1245184 | tf_op jit(solution)/shard_map/all_to_all | solution.py:299
  35.6 0.0 copy-done.3
  35.6 0.8 dual.1
  36.4 4.9 %all-to-all-done.whole_ref = f32[8,152,128]{2,1,0:T(8,128)S(1)} async-done(((f32[8,152,128]{2,1,0:T(8,128)}), f32[8,152,128]{2,1,0:T(8,128)S(1)}, u32[]{:S(2)}, u32[]{:S(2)}) %all-to-all-start) | async-done | bytes 622624 | tf_op jit(solution)/shard_map/all_to_all | solution.py:299
  41.3 0.1 collective-permute-start.2
  41.4 5.3 %collective-permute-start.3 = (f32[152,128]{1,0:T(8,128)S(1)}, f32[152,128]{1,0:T(8,128)S(1)}, u32[]{:S(2)}, u32[]{:S(2)}) collective-permute-start(f32[152,128]{1,0:T(8,128)S(1)} %update.2.x_own.x_ref), channel_id=1, source_target_pairs={{0,248},{1,249},{2,250},{3,251},{4,252},{5,253},{6,254},{7,255},{8... | collective-permute-start | bytes 233480 | tf_op jit(solution)/shard_map/ppermute | solution.py:36
  46.8 0.8 %collective-permute-start.4 = (f32[8,128]{1,0:T(8,128)S(1)}, f32[8,128]{1,0:T(8,128)S(1)}, u32[]{:S(2)}, u32[]{:S(2)}) collective-permute-start(f32[8,128]{1,0:T(8,128)S(1)} %slice.44), channel_id=1, source_target_pairs={{0,240},{1,241},{2,242},{3,243},{4,244},{5,245},{6,246},{7,247},{8... | collective-permute-start | bytes 12296 | tf_op jit(solution)/shard_map/ppermute | solution.py:36
  47.6 2.8 %collective-permute-done.4 = f32[8,128]{1,0:T(8,128)S(1)} collective-permute-done((f32[8,128]{1,0:T(8,128)S(1)}, f32[8,128]{1,0:T(8,128)S(1)}, u32[]{:S(2)}, u32[]{:S(2)}) %collective-permute-start.4) | collective-permute-done | bytes 4128 | tf_op jit(solution)/shard_map/ppermute | solution.py:36
  50.4 0.0 collective-permute-done.2.x_lo
  50.4 0.0 collective-permute-done.3.x_hi
  50.4 3.2 %collective-permute-start.5 = (f32[8,128]{1,0:T(8,128)S(1)}, f32[8,128]{1,0:T(8,128)S(1)}, u32[]{:S(2)}, u32[]{:S(2)}) collective-permute-start(f32[8,128]{1,0:T(8,128)S(1)} %fusion.1), channel_id=1, source_target_pairs={{16,0},{49,1},{82,2},{115,3},{148,4},{181,5},{214,6},{247,7},{24,8... | collective-permute-start | bytes 12296 | tf_op jit(solution)/shard_map/ppermute | solution.py:314
  53.6 0.0 copy-done.9
  53.6 1.3 %copy-done.11 = bf16[2304,256]{1,0:T(8,128)(2,1)S(1)} copy-done((bf16[2304,256]{1,0:T(8,128)(2,1)S(1)}, bf16[2304,256]{1,0:T(8,128)(2,1)}, u32[]{:S(2)}) %copy-start.11) | copy-done | bytes 1179672
  54.9 1.2 %copy-done.13 = f32[128,2048]{1,0:T(8,128)S(1)} copy-done((f32[128,2048]{1,0:T(8,128)S(1)}, f32[128,2048]{1,0:T(8,128)}, u32[]{:S(2)}) %copy-start.13) | copy-done | bytes 1048600
  56.1 5.2 %partial_gradient.3 = f32[8,152,128]{2,1,0:T(8,128)S(1)} custom-call(f32[1]{0:T(128)} %bitcast.20.clip_ref, bf16[2080,128]{1,0:T(8,128)(2,1)S(1)} %collective-permute-done.lo_ref, bf16[2080,128]{1,0:T(8,128)(2,1)S(1)} %collective-permute-done.1.hi_ref, f32[152,128]{1,0:T(8,128)S(1)} %collective-permute-done.2.x_lo, f32[152,128]{1,0:T(8,128)S(1)} %update.2.x_own.x_ref, ...), custom_call_target="tpu_custom_call" | custom-call | flops 3000000000 | bytes 4907008 | tf_op jit(solution)/shard_map/partial_gradient/pallas_call | solution.py:227
  61.3 0.0 collective-permute-done.5
  61.3 14.8 %all_to_all.10.whole_ref = f32[8,152,128]{2,1,0:T(8,128)S(1)} all-to-all(f32[8,152,128]{2,1,0:T(8,128)S(1)} %broadcast_dynamic-update-slice_fusion), channel_id=1, replica_groups=mesh['tile_0'=2,'tile_1'=8,'tile_2'=2,'wave_0'=2,'wave_1'=4] {'wave_0','..., dimensions={0} | all-to-all | bytes 1245184 | tf_op jit(solution)/shard_map/all_to_all | solution.py:325
  76.1 0.1 update.3
  76.2 0.6 slice.46
  76.8 0.6 slice_reduce_fusion
  (19 shorter events, 0.1 us)
Async XLA Ops:
  0.6 0.9 %copy-start = (f32[9,16,128]{2,1,0:T(8,128)S(1)}, f32[9,16,128]{2,1,0:T(8,128)}, u32[]{:S(2)}) copy-start(f32[9,16,128]{2,1,0:T(8,128)} %x_ref.3) | copy-start | bytes 221188
  1.5 0.9 %copy-start.2 = (f32[2,9,16,128]{3,2,1,0:T(8,128)S(1)}, f32[2,9,16,128]{3,2,1,0:T(8,128)}, u32[]{:S(2)}) copy-start(f32[2,9,16,128]{3,2,1,0:T(8,128)} %dual_ref.3) | copy-start | bytes 442372
  2.4 1.0 %copy-start.4 = (bf16[4,32,16,128]{3,2,1,0:T(8,128)(2,1)S(1)}, bf16[4,32,16,128]{3,2,1,0:T(8,128)(2,1)}, u32[]{:S(2)}) copy-start(bf16[4,32,16,128]{3,2,1,0:T(8,128)(2,1)} %param.16) | copy-start | bytes 1572868
  3.5 0.9 %copy-start.6 = (bf16[4,9,16,128]{3,2,1,0:T(8,128)(2,1)S(1)}, bf16[4,9,16,128]{3,2,1,0:T(8,128)(2,1)}, u32[]{:S(2)}) copy-start(bf16[4,9,16,128]{3,2,1,0:T(8,128)(2,1)} %param.14) | copy-start | bytes 442372
  4.4 8.4 %copy-start.14 = (bf16[17,17]{1,0:T(8,128)(2,1)S(1)}, bf16[17,17]{1,0:T(8,128)(2,1)}, u32[]{:S(2)}) copy-start(bf16[17,17]{1,0:T(8,128)(2,1)} %param.17) | copy-start | bytes 1738
  4.4 9.1 %copy-start.5 = (bf16[4,32,16,128]{3,2,1,0:T(8,128)(2,1)S(1)}, bf16[4,32,16,128]{3,2,1,0:T(8,128)(2,1)}, u32[]{:S(2)}) copy-start(bf16[4,32,16,128]{3,2,1,0:T(8,128)(2,1)} %param.16) | copy-start | bytes 1572868
  4.5 13.9 %collective-permute-start = (bf16[2080,128]{1,0:T(8,128)(2,1)S(1)}, bf16[2080,128]{1,0:T(8,128)(2,1)S(1)}, u32[]{:S(2)}, u32[]{:S(2)}) collective-permute-start(bf16[2080,128]{1,0:T(8,128)(2,1)S(1)} %get-tuple-element.22), channel_id=1, source_target_pairs={{0,8},{1,9},{2,10},{3,11},{4,12},{5,13},{6,14},{7,15},{8,16},{9,17... | collective-permute-start | bytes 1597448 | tf_op jit(solution)/shard_map/ppermute | solution.py:36
  4.6 13.8 %collective-permute-start.1 = (bf16[2080,128]{1,0:T(8,128)(2,1)S(1)}, bf16[2080,128]{1,0:T(8,128)(2,1)S(1)}, u32[]{:S(2)}, u32[]{:S(2)}) collective-permute-start(bf16[2080,128]{1,0:T(8,128)(2,1)S(1)} %get-tuple-element.23), channel_id=1, source_target_pairs={{0,248},{1,249},{2,250},{3,251},{4,252},{5,253},{6,254},{7,255},{8... | collective-permute-start | bytes 1597448 | tf_op jit(solution)/shard_map/ppermute | solution.py:36
  13.5 5.0 %copy-start.1 = (f32[9,16,128]{2,1,0:T(8,128)S(1)}, f32[9,16,128]{2,1,0:T(8,128)}, u32[]{:S(2)}) copy-start(f32[9,16,128]{2,1,0:T(8,128)} %x_ref.3) | copy-start | bytes 221188
  13.5 5.0 %copy-start.7 = (bf16[4,9,16,128]{3,2,1,0:T(8,128)(2,1)S(1)}, bf16[4,9,16,128]{3,2,1,0:T(8,128)(2,1)}, u32[]{:S(2)}) copy-start(bf16[4,9,16,128]{3,2,1,0:T(8,128)(2,1)} %param.14) | copy-start | bytes 442372
  24.5 1.0 %copy-start.8 = (bf16[2304,256]{1,0:T(8,128)(2,1)}, bf16[2304,256]{1,0:T(8,128)(2,1)S(1)}, u32[]{:S(2)}) copy-start(bf16[2304,256]{1,0:T(8,128)(2,1)S(1)} %get-tuple-element.25.forward_ref) | copy-start | bytes 3538948
  25.5 1.0 %copy-start.10 = (bf16[2304,256]{1,0:T(8,128)(2,1)}, bf16[2304,256]{1,0:T(8,128)(2,1)S(1)}, u32[]{:S(2)}) copy-start(bf16[2304,256]{1,0:T(8,128)(2,1)S(1)} %get-tuple-element.26.adjoint_ref) | copy-start | bytes 3538948
  26.5 1.0 %copy-start.12 = (f32[128,2048]{1,0:T(8,128)}, f32[128,2048]{1,0:T(8,128)S(1)}, u32[]{:S(2)}) copy-start(f32[128,2048]{1,0:T(8,128)S(1)} %get-tuple-element.24.seen_ref) | copy-start | bytes 3145732
  27.5 8.1 %copy-start.3 = (f32[2,9,16,128]{3,2,1,0:T(8,128)S(1)}, f32[2,9,16,128]{3,2,1,0:T(8,128)}, u32[]{:S(2)}) copy-start(f32[2,9,16,128]{3,2,1,0:T(8,128)} %dual_ref.3) | copy-start | bytes 442372
  27.5 13.8 %all-to-all-start = ((f32[8,152,128]{2,1,0:T(8,128)}), f32[8,152,128]{2,1,0:T(8,128)S(1)}, u32[]{:S(2)}, u32[]{:S(2)}) async-start(f32[8,152,128]{2,1,0:T(8,128)} %partial_gradient.2), calls=%async_computation | async-start | bytes 1245184 | tf_op jit(solution)/shard_map/all_to_all | solution.py:299
  33.5 20.0 %copy-start.9 = (bf16[2304,256]{1,0:T(8,128)(2,1)S(1)}, bf16[2304,256]{1,0:T(8,128)(2,1)}, u32[]{:S(2)}) copy-start(bf16[2304,256]{1,0:T(8,128)(2,1)} %copy-done.8) | copy-start | bytes 3538948
  41.3 9.1 %collective-permute-start.2 = (f32[152,128]{1,0:T(8,128)S(1)}, f32[152,128]{1,0:T(8,128)S(1)}, u32[]{:S(2)}, u32[]{:S(2)}) collective-permute-start(f32[152,128]{1,0:T(8,128)S(1)} %update.2.x_own.x_ref), channel_id=1, source_target_pairs={{0,8},{1,9},{2,10},{3,11},{4,12},{5,13},{6,14},{7,15},{8,16},{9,17... | collective-permute-start | bytes 233480 | tf_op jit(solution)/shard_map/ppermute | solution.py:36
  41.4 9.0 %collective-permute-start.3 = (f32[152,128]{1,0:T(8,128)S(1)}, f32[152,128]{1,0:T(8,128)S(1)}, u32[]{:S(2)}, u32[]{:S(2)}) collective-permute-start(f32[152,128]{1,0:T(8,128)S(1)} %update.2.x_own.x_ref), channel_id=1, source_target_pairs={{0,248},{1,249},{2,250},{3,251},{4,252},{5,253},{6,254},{7,255},{8... | collective-permute-start | bytes 233480 | tf_op jit(solution)/shard_map/ppermute | solution.py:36
  46.8 3.6 %collective-permute-start.4 = (f32[8,128]{1,0:T(8,128)S(1)}, f32[8,128]{1,0:T(8,128)S(1)}, u32[]{:S(2)}, u32[]{:S(2)}) collective-permute-start(f32[8,128]{1,0:T(8,128)S(1)} %slice.44), channel_id=1, source_target_pairs={{0,240},{1,241},{2,242},{3,243},{4,244},{5,245},{6,246},{7,247},{8... | collective-permute-start | bytes 12296 | tf_op jit(solution)/shard_map/ppermute | solution.py:36
  50.4 10.9 %collective-permute-start.5 = (f32[8,128]{1,0:T(8,128)S(1)}, f32[8,128]{1,0:T(8,128)S(1)}, u32[]{:S(2)}, u32[]{:S(2)}) collective-permute-start(f32[8,128]{1,0:T(8,128)S(1)} %fusion.1), channel_id=1, source_target_pairs={{16,0},{49,1},{82,2},{115,3},{148,4},{181,5},{214,6},{247,7},{24,8... | collective-permute-start | bytes 12296 | tf_op jit(solution)/shard_map/ppermute | solution.py:314
  53.6 1.3 %copy-start.11 = (bf16[2304,256]{1,0:T(8,128)(2,1)S(1)}, bf16[2304,256]{1,0:T(8,128)(2,1)}, u32[]{:S(2)}) copy-start(bf16[2304,256]{1,0:T(8,128)(2,1)} %copy-done.10) | copy-start | bytes 3538948
  54.8 1.2 %copy-start.13 = (f32[128,2048]{1,0:T(8,128)S(1)}, f32[128,2048]{1,0:T(8,128)}, u32[]{:S(2)}) copy-start(f32[128,2048]{1,0:T(8,128)} %copy-done.12) | copy-start | bytes 3145732
